TPU v7x, 1024 devices: a whole 4x8x16 slice. The times are simulated.
1024 devices in a mesh: group: 64 (over x, z), head: 8 (over y_hi, core), hid: 2 (over y_lo).
Axes of the slice: x: 4, y: 8 (y_hi: 4, y_lo: 2; y = y_hi * 2 + y_lo), z: 16, core: 2. Of those that a mesh axis runs over, the one named last changes fastest.
Arguments:
- tokens: bfloat16 [16384, 5120], P(('group', 'head', 'hid')), may hold values from -6 to 6
- w_query: bfloat16 [5120, 4096], P('group', ('head', 'hid')), may hold values from -0.078125 to 0.078125
- keyval_weight: bfloat16 [5120, 8, 256], P(('group', 'hid'), 'head'), may hold values from -0.078125 to 0.078125
- q_gain: float32 [128], replicated, may hold values from 0.1 to 1.9
- k_gain: float32 [128], replicated, may hold values from 0.1 to 1.9
- segments: int32 [64, 256], P('group'), may hold values from 0 to 3, never falling along the last dimension, each value on 1 to 128 neighbouring positions
Outputs:
- attention: bfloat16 [16384, 4096], P('group', ('head', 'hid'))
- kv_cache: bfloat16 [16384, 8, 256], P('group', 'head')
Inputs may be any that keep to these rules, and one draw needn't show every extreme that they name: `segments`: within each replica's 256 tokens segment numbers never fall; each of the 4 sequences holds 1 to 128 tokens and one holds exactly 128.
All inputs are finite; a program needn't handle non-finite values.
Results may differ from a plain program's by a relative error of at most 0.0068.
Values may be sent and summed in bfloat16 or wider, within the bound.
No kernel may reach another device: no remote copies, remote signals or barrier semaphores. Data moves between devices by JAX's collectives and lax.ppermute only.
A program may use at most 32 MiB of HBM per device.

v0:
```python
import functools
import math

import jax
import jax.numpy as jnp
from jax import lax
from jax.experimental import pallas as pl
from jax.experimental.pallas import tpu as pltpu
from jax.sharding import Mesh, PartitionSpec as P

QUERY_HEADS = 32
KEYVAL_HEADS = 8

theta_base = 1000000.0
epsilon = 1e-06

N_X, N_Z, N_YH, N_CORE, N_YL = 4, 16, 4, 2, 2
VMEM = pl.BlockSpec(memory_space=pltpu.VMEM)
HBM = pl.BlockSpec(memory_space=pltpu.HBM)


def token_places(seg_ids):
    count_total = seg_ids.shape[0]
    before = jnp.sum((seg_ids[None, :] < seg_ids[:, None]).astype(jnp.int32), axis=1)
    return jnp.arange(count_total, dtype=jnp.int32) - before


def norm_rotate(values, gain, cosine, sine):
    mean = jnp.mean(values * values, axis=-1, keepdims=True)
    values = values * lax.rsqrt(mean + epsilon) * gain
    return values * cosine + pltpu.roll(values, values.shape[-1] // 2, 1) * sine


def meet(where, held, steps, weight):
    rows = weight.reshape(-1, weight.shape[-1])
    wide = rows.shape[0]
    start = pl.multiple_of(lax.rem(where[0] + steps, N_X) * wide, wide)
    return jnp.dot(
        held[:, :, :, :, pl.ds(start, wide)].reshape(-1, wide), rows, preferred_element_type=jnp.float32
    )


def order_kernel(whole, held, sems):
    copies = [
        pltpu.make_async_copy(whole.at[:, near, core], held.at[:, core, near], sems.at[core, near])
        for core in range(N_CORE)
        for near in range(N_YL)
    ]
    for copy in copies:
        copy.start()
    for copy in copies:
        copy.wait()


def keyval_kernel(where, held, own, right, left, far, out, weight):
    rows = own.shape[1]
    for half in range(N_YL):

        @pl.when(where[1] == half)
        def _():
            away = (1 - half) * rows
            for n, ref in enumerate((own, left, far, right)):
                weight[n, :, half * rows : half * rows + rows, :] = ref[...]
                weight[n, :, away : away + rows, :] = jnp.zeros_like(ref)

    out[...] = sum(meet(where, held, n, weight[n]) for n in range(N_X))


def query_kernel(where, held, own, right, left, out):
    out[...] = (
        meet(where, held, 0, own[...]) + meet(where, held, N_X - 1, right[...]) + meet(where, held, 1, left[...])
    )


def attend_kernel(head_size, where, held, far, near, own, partner, q_gain, k_gain, cosine, sine, bias, out, cache):
    query = near[...] + meet(where, held, 2, far[...])
    key_value = own[...] + partner[...]
    key_rot = norm_rotate(key_value[:, :head_size], k_gain[...], cosine[...], sine[...]).astype(jnp.bfloat16)
    value_b = key_value[:, head_size:].astype(jnp.bfloat16)
    cache[:, :head_size] = key_rot
    cache[:, head_size:] = value_b
    for h in range(out.shape[1] // head_size):
        span = slice(h * head_size, (h + 1) * head_size)
        query_rot = norm_rotate(query[:, span], q_gain[...], cosine[...], sine[...]).astype(jnp.bfloat16)
        scores = lax.dot_general(
            query_rot, key_rot, (((1,), (1,)), ((), ())), preferred_element_type=jnp.float32
        ) / math.sqrt(head_size)
        masked = scores + bias[...]
        expd = jnp.exp(masked - jnp.max(masked, axis=-1, keepdims=True))
        probs = (expd / jnp.sum(expd, axis=-1, keepdims=True)).astype(jnp.bfloat16)
        out[:, span] = jnp.dot(probs, value_b, preferred_element_type=jnp.float32).astype(jnp.bfloat16)


def body(tokens, w_query, keyval_weight, q_gain, k_gain, segments):
    q_rows, q_cols = w_query.shape
    kv_rows, _, pair_width = keyval_weight.shape
    head_size = pair_width // 2
    where = jnp.stack([lax.axis_index(axis) for axis in ("x", "yl")]).astype(jnp.int32)

    pair = lax.all_gather(tokens, "core", axis=0, tiled=True)
    whole = lax.all_gather(pair, ("yh", "yl"), axis=0, tiled=True)

    seg_ids = segments.reshape(-1)
    count_total = seg_ids.shape[0]
    half = head_size // 2
    freqs = jnp.power(theta_base, -2.0 * jnp.arange(half, dtype=jnp.float32) / head_size)
    angles = token_places(seg_ids).astype(jnp.float32)[:, None] * freqs[None, :]
    cosine, sine = jnp.cos(angles), jnp.sin(angles)
    cosine = jnp.concatenate([cosine, cosine], axis=1)
    sine = jnp.concatenate([-sine, sine], axis=1)

    index = jnp.arange(count_total, dtype=jnp.int32)
    allowed = (index[None, :] <= index[:, None]) & (seg_ids[None, :] == seg_ids[:, None])
    bias = jnp.where(allowed, jnp.float32(0.0), jnp.float32(-1e30))

    block = jnp.concatenate([w_query, keyval_weight.reshape(kv_rows, pair_width)], axis=0)
    column = lax.all_gather(block, "z", axis=0)
    query_own, key_own = column[:, :q_rows], column[:, q_rows:]

    def up(a):
        return lax.ppermute(a, "x", [(x, (x + 1) % N_X) for x in range(N_X)])

    def down(a):
        return lax.ppermute(a, "x", [(x, (x - 1) % N_X) for x in range(N_X)])

    key_right, query_left = up(key_own), down(query_own)
    query_right, key_left = up(query_own), down(key_own)
    key_right, where, cosine, sine, bias = lax.optimization_barrier((key_right, where, cosine, sine, bias))
    key_far, query_far = up(key_right), down(query_left)
    query_right, key_left, key_right, whole = lax.optimization_barrier((query_right, key_left, key_right, whole))
    depth = N_X * N_Z * q_rows
    held = pl.pallas_call(
        order_kernel,
        out_shape=jax.ShapeDtypeStruct((N_YH, N_CORE, N_YL, tokens.shape[0], depth), jnp.bfloat16),
        in_specs=[HBM],
        out_specs=VMEM,
        scratch_shapes=[pltpu.SemaphoreType.DMA((N_CORE, N_YL))],
        cost_estimate=pl.CostEstimate(flops=0, bytes_accessed=4 * count_total * depth, transcendentals=0),
        compiler_params=pltpu.CompilerParams(vmem_limit_bytes=16 << 20),
    )(pltpu.with_memory_space_constraint(whole.reshape(N_YH, N_YL, N_CORE, tokens.shape[0], depth), pltpu.HBM))

    smem = pl.BlockSpec(memory_space=pltpu.SMEM)

    def settings(slots):
        return dict(
            cost_estimate=pl.CostEstimate(
                flops=2 * slots * count_total * (depth // N_X) * q_cols,
                bytes_accessed=2 * slots * (depth // N_X) * (q_cols + count_total),
                transcendentals=0,
            ),
            compiler_params=pltpu.CompilerParams(vmem_limit_bytes=16 << 20),
        )

    partial = pl.pallas_call(
        keyval_kernel,
        out_shape=jax.ShapeDtypeStruct((count_total, pair_width), jnp.float32),
        in_specs=[smem, *[VMEM] * 5],
        out_specs=VMEM,
        scratch_shapes=[pltpu.VMEM((N_X, N_Z, q_rows, q_cols), jnp.bfloat16)],
        **settings(N_X),
    )(where, held, key_own, key_right, key_left, key_far)
    partner = lax.ppermute(partial, "yl", [(0, 1), (1, 0)])
    near = pl.pallas_call(
        query_kernel,
        out_shape=jax.ShapeDtypeStruct((count_total, q_cols), jnp.float32),
        in_specs=[smem, *[VMEM] * 4],
        out_specs=VMEM,
        **settings(N_X - 1),
    )(where, held, query_own, query_right, query_left)
    attention, cache = pl.pallas_call(
        functools.partial(attend_kernel, head_size),
        out_shape=(
            jax.ShapeDtypeStruct((count_total, q_cols), jnp.bfloat16),
            jax.ShapeDtypeStruct((count_total, pair_width), jnp.bfloat16),
        ),
        in_specs=[smem, *[VMEM] * 10],
        out_specs=(VMEM, VMEM),
        **settings(1),
    )(where, held, query_far, near, partial, partner, q_gain[None], k_gain[None], cosine, sine, bias)
    return attention, cache[:, None, :]


def solution(mesh):
    fine = Mesh(
        mesh.devices.reshape(N_X, N_Z, N_YH, N_CORE, N_YL), ("x", "z", "yh", "core", "yl")
    )
    group, head = ("x", "z"), ("yh", "core")
    return jax.shard_map(
        body,
        mesh=fine,
        in_specs=(
            P((*group, *head, "yl"), None),
            P(group, (*head, "yl")),
            P((*group, "yl"), head, None),
            P(),
            P(),
            P(group, None),
        ),
        out_specs=(P(group, (*head, "yl")), P(group, head, None)),
        check_vma=False,
    )
```

profile of v0, /device:TPU:32, one launch (start us, length us, event | category | flops | bytes accessed | tf_op | source)
XLA Modules:
  0.0 121.7 jit_solution(15266328583533654122)
XLA Ops:
  7.2 0.0 copy-start.2
  7.2 0.0 all-gather.3.cloned.1.call-start
  7.2 3.6 %all_gather.14 = bf16[32,5120]{1,0:T(8,128)(2,1)} all-gather(bf16[16,5120]{1,0:T(8,128)(2,1)} %param.6), channel_id=1, replica_groups=mesh['x'=4,'z'=16,'yh'=4,'core'=2,'yl'=2] {'core'}, dimensions={0}, use_global_device_ids=true | all-gather | bytes 491520 | tf_op jit(solution)/shard_map/all_gather | solution.py:100
  10.8 0.0 all-gather.3.cloned.1.call-update
  10.8 0.8 pad_maximum_fusion.2
  11.6 48.0 %all-gather = bf16[1920,256]{1,0:T(8,128)(2,1)S(1)} all-gather(bf16[120,256]{1,0:T(8,128)(2,1)S(1)} %pad_maximum_fusion.2), channel_id=2, replica_groups=mesh['x'=4,'z'=16,'yh'=4,'core'=2,'yl'=2] {'z'}, dimensions={0}, use_global_device_ids=true | all-gather | bytes 1044480 | tf_op jit(solution)/shard_map/all_gather | solution.py:117
  59.7 3.4 %collective-permute-start = (bf16[16,40,256]{2,1,0:T(8,128)(2,1)S(1)}, bf16[16,40,256]{2,1,0:T(8,128)(2,1)}, u32[]{:S(2)}, u32[]{:S(2)}) collective-permute-start(bf16[16,40,256]{2,1,0:T(8,128)(2,1)S(1)} %slice.8.own), channel_id=1, source_target_pairs={{0,256},{256,512},{512,768},{768,0},{1,257},{257,513},{513,769},{7... | collective-permute-start | bytes 983048 | tf_op jit(solution)/shard_map/ppermute | solution.py:121
  63.1 3.7 %collective-permute-start.2 = (bf16[16,40,256]{2,1,0:T(8,128)(2,1)S(1)}, bf16[16,40,256]{2,1,0:T(8,128)(2,1)}, u32[]{:S(2)}, u32[]{:S(2)}) collective-permute-start(bf16[16,40,256]{2,1,0:T(8,128)(2,1)S(1)} %slice.8.own), channel_id=1, source_target_pairs={{0,768},{256,0},{512,256},{768,512},{1,769},{257,1},{513,257},{769... | collective-permute-start | bytes 983048 | tf_op jit(solution)/shard_map/ppermute | solution.py:124
  66.8 2.2 %collective-permute-start.1 = (bf16[16,80,256]{2,1,0:T(8,128)(2,1)S(1)}, bf16[16,80,256]{2,1,0:T(8,128)(2,1)S(1)}, u32[]{:S(2)}, u32[]{:S(2)}) collective-permute-start(bf16[16,80,256]{2,1,0:T(8,128)(2,1)S(1)} %slice.9.own), channel_id=1, source_target_pairs={{0,256},{256,512},{512,768},{768,0},{1,257},{257,513},{513,769},{7... | collective-permute-start | bytes 1966088 | tf_op jit(solution)/shard_map/ppermute | solution.py:121
  69.0 4.9 %collective-permute-start.3 = (bf16[16,80,256]{2,1,0:T(8,128)(2,1)S(1)}, bf16[16,80,256]{2,1,0:T(8,128)(2,1)S(1)}, u32[]{:S(2)}, u32[]{:S(2)}) collective-permute-start(bf16[16,80,256]{2,1,0:T(8,128)(2,1)S(1)} %slice.9.own), channel_id=1, source_target_pairs={{0,768},{256,0},{512,256},{768,512},{1,769},{257,1},{513,257},{769... | collective-permute-start | bytes 1966088 | tf_op jit(solution)/shard_map/ppermute | solution.py:124
  73.9 0.0 copy-done.2
  73.9 0.2 convert_reduce_fusion
  74.1 0.5 fusion.2
  74.7 0.1 pad_maximum_fusion
  74.8 0.1 fusion.1.bias
  74.9 10.9 %collective-permute-done.3.left = bf16[16,80,256]{2,1,0:T(8,128)(2,1)S(1)} collective-permute-done((bf16[16,80,256]{2,1,0:T(8,128)(2,1)S(1)}, bf16[16,80,256]{2,1,0:T(8,128)(2,1)S(1)}, u32[]{:S(2)}, u32[]{:S(2)}) %collective-permute-start.3) | collective-permute-done | bytes 655392 | tf_op jit(solution)/shard_map/ppermute | solution.py:124
  85.8 5.1 %collective-permute-start.4 = (bf16[16,80,256]{2,1,0:T(8,128)(2,1)S(1)}, bf16[16,80,256]{2,1,0:T(8,128)(2,1)S(1)}, u32[]{:S(2)}, u32[]{:S(2)}) collective-permute-start(bf16[16,80,256]{2,1,0:T(8,128)(2,1)S(1)} %collective-permute-done.3.left), channel_id=1, source_target_pairs={{0,768},{256,0},{512,256},{768,512},{1,769},{257,1},{513,257},{769... | collective-permute-start | bytes 1966088 | tf_op jit(solution)/shard_map/ppermute | solution.py:124
  91.0 0.1 pad_add_fusion.where
  91.1 0.0 collective-permute-done.right
  91.1 1.9 %collective-permute-start.5 = (bf16[16,40,256]{2,1,0:T(8,128)(2,1)}, bf16[16,40,256]{2,1,0:T(8,128)(2,1)}, u32[]{:S(2)}, u32[]{:S(2)}) collective-permute-start(bf16[16,40,256]{2,1,0:T(8,128)(2,1)} %collective-permute-done.right), channel_id=1, source_target_pairs={{0,256},{256,512},{512,768},{768,0},{1,257},{257,513},{513,769},{7... | collective-permute-start | bytes 983048 | tf_op jit(solution)/shard_map/ppermute | solution.py:121
  93.0 0.0 collective-permute-done.2.left
  93.0 0.0 collective-permute-done.1.right
  93.0 0.0 all-gather.3.cloned.1.call-done
  93.1 1.7 %shard_map.77.held = bf16[4,2,2,16,5120]{4,3,2,1,0:T(8,128)(2,1)S(1)} custom-call(bf16[4,2,2,16,5120]{4,3,2,1,0:T(8,128)(2,1)} %bitcast.13), custom_call_target="tpu_custom_call" | custom-call | bytes 5242880 | tf_op jit(solution)/shard_map/pallas_call | solution.py:132
  94.8 6.8 %collective-permute-done.5.far = bf16[16,40,256]{2,1,0:T(8,128)(2,1)} collective-permute-done((bf16[16,40,256]{2,1,0:T(8,128)(2,1)}, bf16[16,40,256]{2,1,0:T(8,128)(2,1)}, u32[]{:S(2)}, u32[]{:S(2)}) %collective-permute-start.5) | collective-permute-done | bytes 327712 | tf_op jit(solution)/shard_map/ppermute | solution.py:121
  101.6 2.2 %shard_map.79.own = f32[256,256]{1,0:T(8,128)S(1)} custom-call(s32[2]{0:T(128)S(1)} %pad_add_fusion.where, bf16[4,2,2,16,5120]{4,3,2,1,0:T(8,128)(2,1)S(1)} %shard_map.77.held, bf16[16,40,256]{2,1,0:T(8,128)(2,1)S(1)} %slice.8.own, bf16[16,40,256]{2,1,0:T(8,128)(2,1)} %collective-permute-done.right, bf16[16,40,256]{2,1,0:T(8,128)(2,1)} %collective-permute-done.2.left, ...), custom_call_target="tpu_custom_call" | custom-call | flops 671088640 | bytes 5242880 | tf_op jit(solution)/shard_map/pallas_call | solution.py:154
  103.8 0.0 copy-start
  103.8 0.0 copy-start.1
  103.8 1.9 %collective-permute-start.6 = (f32[256,256]{1,0:T(8,128)S(1)}, f32[256,256]{1,0:T(8,128)S(1)}, u32[]{:S(2)}, u32[]{:S(2)}) collective-permute-start(f32[256,256]{1,0:T(8,128)S(1)} %shard_map.79.own), channel_id=1, source_target_pairs={{0,1},{1,0},{2,3},{3,2},{4,5},{5,4},{6,7},{7,6},{8,9},{9,8},{10,11... | collective-permute-start | bytes 786440 | tf_op jit(solution)/shard_map/ppermute | solution.py:162
  105.8 1.2 %shard_map.78.near = f32[256,256]{1,0:T(8,128)S(1)} custom-call(s32[2]{0:T(128)S(1)} %pad_add_fusion.where, bf16[4,2,2,16,5120]{4,3,2,1,0:T(8,128)(2,1)S(1)} %shard_map.77.held, bf16[16,80,256]{2,1,0:T(8,128)(2,1)S(1)} %slice.9.own, bf16[16,80,256]{2,1,0:T(8,128)(2,1)S(1)} %collective-permute-done.1.right, bf16[16,80,256]{2,1,0:T(8,128)(2,1)S(1)} %collective-permute-done.3.left), custom_call_target="tpu_custom_call" | custom-call | flops 503316480 | bytes 3932160 | tf_op jit(solution)/shard_map/pallas_call | solution.py:163
  107.0 0.0 collective-permute-done.4.far
  107.0 5.1 %collective-permute-done.6.partner = f32[256,256]{1,0:T(8,128)S(1)} collective-permute-done((f32[256,256]{1,0:T(8,128)S(1)}, f32[256,256]{1,0:T(8,128)S(1)}, u32[]{:S(2)}, u32[]{:S(2)}) %collective-permute-start.6) | collective-permute-done | bytes 262176 | tf_op jit(solution)/shard_map/ppermute | solution.py:162
  112.1 0.0 copy-done
  112.1 0.0 copy-done.1
  112.1 2.7 %shard_map.80 = (bf16[256,256]{1,0:T(8,128)(2,1)}, bf16[256,256]{1,0:T(8,128)(2,1)}) custom-call(s32[2]{0:T(128)S(1)} %pad_add_fusion.where, bf16[4,2,2,16,5120]{4,3,2,1,0:T(8,128)(2,1)S(1)} %shard_map.77.held, bf16[16,80,256]{2,1,0:T(8,128)(2,1)S(1)} %collective-permute-done.4.far, f32[256,256]{1,0:T(8,128)S(1)} %shard_map.78.near, ...), custom_call_target="tpu_custom_call" | custom-call | flops 167772160 | bytes 1310720 | tf_op jit(solution)/shard_map/pallas_call | solution.py:170
  (4 shorter events, 0.1 us)
Async XLA Ops:
  7.2 66.8 %copy-start.2 = (s32[1,256]{1,0:T(1,128)S(1)}, s32[1,256]{1,0:T(1,128)}, u32[]{:S(2)}) copy-start(s32[1,256]{1,0:T(1,128)} %param.11) | copy-start | bytes 3076
  7.2 85.9 %all-gather.3.cloned.1.call-start = ((), (), s32[]{:S(2)}) async-start(), calls=%async_computation | async-start | bytes 2949120 | tf_op jit(solution)/shard_map/all_gather | solution.py:101
  59.7 31.4 %collective-permute-start = (bf16[16,40,256]{2,1,0:T(8,128)(2,1)S(1)}, bf16[16,40,256]{2,1,0:T(8,128)(2,1)}, u32[]{:S(2)}, u32[]{:S(2)}) collective-permute-start(bf16[16,40,256]{2,1,0:T(8,128)(2,1)S(1)} %slice.8.own), channel_id=1, source_target_pairs={{0,256},{256,512},{512,768},{768,0},{1,257},{257,513},{513,769},{7... | collective-permute-start | bytes 983048 | tf_op jit(solution)/shard_map/ppermute | solution.py:121
  63.1 29.9 %collective-permute-start.2 = (bf16[16,40,256]{2,1,0:T(8,128)(2,1)S(1)}, bf16[16,40,256]{2,1,0:T(8,128)(2,1)}, u32[]{:S(2)}, u32[]{:S(2)}) collective-permute-start(bf16[16,40,256]{2,1,0:T(8,128)(2,1)S(1)} %slice.8.own), channel_id=1, source_target_pairs={{0,768},{256,0},{512,256},{768,512},{1,769},{257,1},{513,257},{769... | collective-permute-start | bytes 983048 | tf_op jit(solution)/shard_map/ppermute | solution.py:124
  66.8 26.2 %collective-permute-start.1 = (bf16[16,80,256]{2,1,0:T(8,128)(2,1)S(1)}, bf16[16,80,256]{2,1,0:T(8,128)(2,1)S(1)}, u32[]{:S(2)}, u32[]{:S(2)}) collective-permute-start(bf16[16,80,256]{2,1,0:T(8,128)(2,1)S(1)} %slice.9.own), channel_id=1, source_target_pairs={{0,256},{256,512},{512,768},{768,0},{1,257},{257,513},{513,769},{7... | collective-permute-start | bytes 1966088 | tf_op jit(solution)/shard_map/ppermute | solution.py:121
  69.0 16.8 %collective-permute-start.3 = (bf16[16,80,256]{2,1,0:T(8,128)(2,1)S(1)}, bf16[16,80,256]{2,1,0:T(8,128)(2,1)S(1)}, u32[]{:S(2)}, u32[]{:S(2)}) collective-permute-start(bf16[16,80,256]{2,1,0:T(8,128)(2,1)S(1)} %slice.9.own), channel_id=1, source_target_pairs={{0,768},{256,0},{512,256},{768,512},{1,769},{257,1},{513,257},{769... | collective-permute-start | bytes 1966088 | tf_op jit(solution)/shard_map/ppermute | solution.py:124
  85.8 21.2 %collective-permute-start.4 = (bf16[16,80,256]{2,1,0:T(8,128)(2,1)S(1)}, bf16[16,80,256]{2,1,0:T(8,128)(2,1)S(1)}, u32[]{:S(2)}, u32[]{:S(2)}) collective-permute-start(bf16[16,80,256]{2,1,0:T(8,128)(2,1)S(1)} %collective-permute-done.3.left), channel_id=1, source_target_pairs={{0,768},{256,0},{512,256},{768,512},{1,769},{257,1},{513,257},{769... | collective-permute-start | bytes 1966088 | tf_op jit(solution)/shard_map/ppermute | solution.py:124
  91.1 10.5 %collective-permute-start.5 = (bf16[16,40,256]{2,1,0:T(8,128)(2,1)}, bf16[16,40,256]{2,1,0:T(8,128)(2,1)}, u32[]{:S(2)}, u32[]{:S(2)}) collective-permute-start(bf16[16,40,256]{2,1,0:T(8,128)(2,1)} %collective-permute-done.right), channel_id=1, source_target_pairs={{0,256},{256,512},{512,768},{768,0},{1,257},{257,513},{513,769},{7... | collective-permute-start | bytes 983048 | tf_op jit(solution)/shard_map/ppermute | solution.py:121
  103.8 8.3 %copy-start = (f32[128]{0:T(128)S(1)}, f32[128]{0:T(128)}, u32[]{:S(2)}) copy-start(f32[128]{0:T(128)} %param.9) | copy-start | bytes 1540
  103.8 8.3 %copy-start.1 = (f32[128]{0:T(128)S(1)}, f32[128]{0:T(128)}, u32[]{:S(2)}) copy-start(f32[128]{0:T(128)} %param.10) | copy-start | bytes 1540
  103.8 8.3 %collective-permute-start.6 = (f32[256,256]{1,0:T(8,128)S(1)}, f32[256,256]{1,0:T(8,128)S(1)}, u32[]{:S(2)}, u32[]{:S(2)}) collective-permute-start(f32[256,256]{1,0:T(8,128)S(1)} %shard_map.79.own), channel_id=1, source_target_pairs={{0,1},{1,0},{2,3},{3,2},{4,5},{5,4},{6,7},{7,6},{8,9},{9,8},{10,11... | collective-permute-start | bytes 786440 | tf_op jit(solution)/shard_map/ppermute | solution.py:162
Sparse Core Ops, SparseCore 0:
  11.0 55.1 all-gather.2
where the time goes:
time: 122 us
  blocking collectives  51.6 us (42%)
  starting transfers between devices  23.1 us (19%)
  waiting for transfers between devices  22.8 us (19%)
  between operations  14.2 us (12%)
  Pallas kernels  7.9 us (6%)
  other arithmetic  1.85 us (2%)
    all_gather x1, blocking collectives, body(): column = lax.all_gather(block, 'z', axis=0)  48 us
    ppermute x3, starting transfers between devices, down(): return lax.ppermute(a, 'x', [(x, (x - 1) % N_X) for x in range(N_X)])  13.7 us
    ppermute x3, waiting for transfers between devices, down(): return lax.ppermute(a, 'x', [(x, (x - 1) % N_X) for x in range(N_X)])  10.9 us
    ppermute x3, starting transfers between devices, up(): return lax.ppermute(a, 'x', [(x, (x + 1) % N_X) for x in range(N_X)])  7.5 us
    ppermute x3, waiting for transfers between devices, up(): return lax.ppermute(a, 'x', [(x, (x + 1) % N_X) for x in range(N_X)])  6.8 us
    ppermute x1, waiting for transfers between devices, body(): partner = lax.ppermute(partial, 'yl', [(0, 1), (1, 0)])  5.09 us
    all_gather x1, blocking collectives, body(): pair = lax.all_gather(tokens, 'core', axis=0, tiled=True)  3.6 us
    pallas_call x1, Pallas kernels, body(): pl.pallas_call(functools.partial(attend_kernel, head_size), out_shape=(ja...  2.71 us
  transfers between devices with their start and end apart: 8, of which 3 were waited for; matrix products, arithmetic and copies ran while one was open for 2% of the time, Pallas kernels for 4%

commit v1 on v0

--- a/solution.py
+++ b/solution.py
@@ -115,19 +115,21 @@
 
     block = jnp.concatenate([w_query, keyval_weight.reshape(kv_rows, pair_width)], axis=0)
     column = lax.all_gather(block, "z", axis=0)
-    query_own, key_own = column[:, :q_rows], column[:, q_rows:]
-
     def up(a):
         return lax.ppermute(a, "x", [(x, (x + 1) % N_X) for x in range(N_X)])
 
     def down(a):
         return lax.ppermute(a, "x", [(x, (x - 1) % N_X) for x in range(N_X)])
 
-    key_right, query_left = up(key_own), down(query_own)
-    query_right, key_left = up(query_own), down(key_own)
-    key_right, where, cosine, sine, bias = lax.optimization_barrier((key_right, where, cosine, sine, bias))
-    key_far, query_far = up(key_right), down(query_left)
-    query_right, key_left, key_right, whole = lax.optimization_barrier((query_right, key_left, key_right, whole))
+    query_left = down(column[:, :q_rows])
+    column, where, cosine, sine, bias = lax.optimization_barrier((column, where, cosine, sine, bias))
+    key_own = column[:, q_rows:]
+    key_right, key_left = up(key_own), down(key_own)
+    column, key_right = lax.optimization_barrier((column, key_right))
+    query_own = column[:, :q_rows]
+    query_right = up(query_own)
+    key_far = up(key_right)
+    whole, key_right = lax.optimization_barrier((whole, key_right))
     depth = N_X * N_Z * q_rows
     held = pl.pallas_call(
         order_kernel,
@@ -135,17 +137,19 @@
         in_specs=[HBM],
         out_specs=VMEM,
         scratch_shapes=[pltpu.SemaphoreType.DMA((N_CORE, N_YL))],
-        cost_estimate=pl.CostEstimate(flops=0, bytes_accessed=4 * count_total * depth, transcendentals=0),
+        cost_estimate=pl.CostEstimate(flops=0, bytes_accessed=10 * 4 * count_total * depth, transcendentals=0),
         compiler_params=pltpu.CompilerParams(vmem_limit_bytes=16 << 20),
     )(pltpu.with_memory_space_constraint(whole.reshape(N_YH, N_YL, N_CORE, tokens.shape[0], depth), pltpu.HBM))
 
+    query_left, held = lax.optimization_barrier((query_left, held))
+    query_far = down(query_left)
     smem = pl.BlockSpec(memory_space=pltpu.SMEM)
 
     def settings(slots):
         return dict(
             cost_estimate=pl.CostEstimate(
-                flops=2 * slots * count_total * (depth // N_X) * q_cols,
-                bytes_accessed=2 * slots * (depth // N_X) * (q_cols + count_total),
+                flops=10 * 2 * slots * count_total * (depth // N_X) * q_cols,
+                bytes_accessed=10 * 2 * slots * (depth // N_X) * (q_cols + count_total),
                 transcendentals=0,
             ),
             compiler_params=pltpu.CompilerParams(vmem_limit_bytes=16 << 20),

time: 122 us -> 111 us (0.910)
  the two profiles are of different devices: /device:TPU:32 before, /device:TPU:40 now
where the time goes in v1:
time: 111 us
  blocking collectives  51.7 us (47%)
  starting transfers between devices  23.7 us (21%)
  between operations  14.2 us (13%)
  waiting for transfers between devices  9.39 us (8%)
  Pallas kernels  7.7 us (7%)
  local copies, waits for them, and re-layouts  2.11 us (2%)
  other arithmetic  1.85 us (2%)
    all_gather x1, blocking collectives, body(): column = lax.all_gather(block, 'z', axis=0)  48 us
    ppermute x3, starting transfers between devices, down(): return lax.ppermute(a, 'x', [(x, (x - 1) % N_X) for x in range(N_X)])  14.5 us
    ppermute x3, waiting for transfers between devices, up(): return lax.ppermute(a, 'x', [(x, (x + 1) % N_X) for x in range(N_X)])  7.17 us
    ppermute x3, starting transfers between devices, up(): return lax.ppermute(a, 'x', [(x, (x + 1) % N_X) for x in range(N_X)])  6.19 us
    all_gather x1, blocking collectives, body(): pair = lax.all_gather(tokens, 'core', axis=0, tiled=True)  3.61 us
    ppermute x1, starting transfers between devices, body(): partner = lax.ppermute(partial, 'yl', [(0, 1), (1, 0)])  3.04 us
    pallas_call x1, Pallas kernels, body(): pl.pallas_call(functools.partial(attend_kernel, head_size), out_shape=(ja...  2.72 us
  transfers between devices with their start and end apart: 8, of which 4 were waited for; matrix products, arithmetic and copies ran while one was open for 4% of the time, Pallas kernels for 4%

profile of v1, /device:TPU:40, one launch (start us, length us, event | category | flops | bytes accessed | tf_op | source)
XLA Modules:
  0.0 110.7 jit_solution(6594810644461206315)
XLA Ops:
  7.2 0.0 copy-start.3
  7.2 0.0 all-gather.3.cloned.1.call-start
  7.2 3.6 %all_gather.14 = bf16[32,5120]{1,0:T(8,128)(2,1)} all-gather(bf16[16,5120]{1,0:T(8,128)(2,1)} %param.6), channel_id=1, replica_groups=mesh['x'=4,'z'=16,'yh'=4,'core'=2,'yl'=2] {'core'}, dimensions={0}, use_global_device_ids=true | all-gather | bytes 491520 | tf_op jit(solution)/shard_map/all_gather | solution.py:100
  10.8 0.0 all-gather.3.cloned.1.call-update
  10.9 0.8 pad_maximum_fusion.2
  11.7 48.0 %all-gather = bf16[1920,256]{1,0:T(8,128)(2,1)S(1)} all-gather(bf16[120,256]{1,0:T(8,128)(2,1)S(1)} %pad_maximum_fusion.2), channel_id=2, replica_groups=mesh['x'=4,'z'=16,'yh'=4,'core'=2,'yl'=2] {'z'}, dimensions={0}, use_global_device_ids=true | all-gather | bytes 1044480 | tf_op jit(solution)/shard_map/all_gather | solution.py:117
  59.7 0.0 copy-start.2
  59.7 0.9 slice.12
  60.6 4.7 %collective-permute-start = (bf16[16,80,256]{2,1,0:T(8,128)(2,1)}, bf16[16,80,256]{2,1,0:T(8,128)(2,1)S(1)}, u32[]{:S(2)}, u32[]{:S(2)}) collective-permute-start(bf16[16,80,256]{2,1,0:T(8,128)(2,1)} %slice.12), channel_id=1, source_target_pairs={{0,768},{256,0},{512,256},{768,512},{1,769},{257,1},{513,257},{769... | collective-permute-start | bytes 1966088 | tf_op jit(solution)/shard_map/ppermute | solution.py:122
  65.3 0.1 pad_add_fusion.where
  65.4 0.0 copy-done.3
  65.4 0.2 convert_reduce_fusion
  65.6 0.5 fusion.2
  66.1 0.1 pad_maximum_fusion
  66.3 0.1 fusion.1.bias
  66.4 0.0 copy-done.2
  66.4 1.9 %collective-permute-start.1 = (bf16[16,40,256]{2,1,0:T(8,128)(2,1)S(1)}, bf16[16,40,256]{2,1,0:T(8,128)(2,1)S(1)}, u32[]{:S(2)}, u32[]{:S(2)}) collective-permute-start(bf16[16,40,256]{2,1,0:T(8,128)(2,1)S(1)} %slice.10.own), channel_id=1, source_target_pairs={{0,256},{256,512},{512,768},{768,0},{1,257},{257,513},{513,769},{7... | collective-permute-start | bytes 983048 | tf_op jit(solution)/shard_map/ppermute | solution.py:119
  68.4 5.1 %collective-permute-start.4 = (bf16[16,40,256]{2,1,0:T(8,128)(2,1)S(1)}, bf16[16,40,256]{2,1,0:T(8,128)(2,1)S(1)}, u32[]{:S(2)}, u32[]{:S(2)}) collective-permute-start(bf16[16,40,256]{2,1,0:T(8,128)(2,1)S(1)} %slice.10.own), channel_id=1, source_target_pairs={{0,768},{256,0},{512,256},{768,512},{1,769},{257,1},{513,257},{769... | collective-permute-start | bytes 983048 | tf_op jit(solution)/shard_map/ppermute | solution.py:122
  73.5 5.0 %collective-permute-done.1.right = bf16[16,40,256]{2,1,0:T(8,128)(2,1)S(1)} collective-permute-done((bf16[16,40,256]{2,1,0:T(8,128)(2,1)S(1)}, bf16[16,40,256]{2,1,0:T(8,128)(2,1)S(1)}, u32[]{:S(2)}, u32[]{:S(2)}) %collective-permute-start.1) | collective-permute-done | bytes 327712 | tf_op jit(solution)/shard_map/ppermute | solution.py:119
  78.5 1.9 %collective-permute-start.5 = (bf16[16,40,256]{2,1,0:T(8,128)(2,1)S(1)}, bf16[16,40,256]{2,1,0:T(8,128)(2,1)}, u32[]{:S(2)}, u32[]{:S(2)}) collective-permute-start(bf16[16,40,256]{2,1,0:T(8,128)(2,1)S(1)} %collective-permute-done.1.right), channel_id=1, source_target_pairs={{0,256},{256,512},{512,768},{768,0},{1,257},{257,513},{513,769},{7... | collective-permute-start | bytes 983048 | tf_op jit(solution)/shard_map/ppermute | solution.py:119
  80.4 1.1 %slice.11.own = bf16[16,80,256]{2,1,0:T(8,128)(2,1)S(1)} slice(bf16[16,120,256]{2,1,0:T(8,128)(2,1)} %bitcast.13), slice={[0:16], [0:80], [0:256]} | slice | bytes 1310720 | tf_op jit(solution)/shard_map/slice | solution.py:129
  81.5 2.4 %collective-permute-start.3 = (bf16[16,80,256]{2,1,0:T(8,128)(2,1)S(1)}, bf16[16,80,256]{2,1,0:T(8,128)(2,1)S(1)}, u32[]{:S(2)}, u32[]{:S(2)}) collective-permute-start(bf16[16,80,256]{2,1,0:T(8,128)(2,1)S(1)} %slice.11.own), channel_id=1, source_target_pairs={{0,256},{256,512},{512,768},{768,0},{1,257},{257,513},{513,769},{7... | collective-permute-start | bytes 1966088 | tf_op jit(solution)/shard_map/ppermute | solution.py:119
  83.9 0.0 all-gather.3.cloned.1.call-done
  83.9 1.7 %shard_map.77.held = bf16[4,2,2,16,5120]{4,3,2,1,0:T(8,128)(2,1)S(1)} custom-call(bf16[4,2,2,16,5120]{4,3,2,1,0:T(8,128)(2,1)} %bitcast.14), custom_call_target="tpu_custom_call" | custom-call | bytes 52428800 | tf_op jit(solution)/shard_map/pallas_call | solution.py:134
  85.7 0.0 collective-permute-done.left
  85.7 4.7 %collective-permute-start.2 = (bf16[16,80,256]{2,1,0:T(8,128)(2,1)S(1)}, bf16[16,80,256]{2,1,0:T(8,128)(2,1)S(1)}, u32[]{:S(2)}, u32[]{:S(2)}) collective-permute-start(bf16[16,80,256]{2,1,0:T(8,128)(2,1)S(1)} %collective-permute-done.left), channel_id=1, source_target_pairs={{0,768},{256,0},{512,256},{768,512},{1,769},{257,1},{513,257},{769... | collective-permute-start | bytes 1966088 | tf_op jit(solution)/shard_map/ppermute | solution.py:122
  90.4 0.0 collective-permute-done.4.left
  90.4 0.4 collective-permute-done.5.far
  90.8 2.0 %shard_map.79.own = f32[256,256]{1,0:T(8,128)S(1)} custom-call(s32[2]{0:T(128)S(1)} %pad_add_fusion.where, bf16[4,2,2,16,5120]{4,3,2,1,0:T(8,128)(2,1)S(1)} %shard_map.77.held, bf16[16,40,256]{2,1,0:T(8,128)(2,1)S(1)} %slice.10.own, bf16[16,40,256]{2,1,0:T(8,128)(2,1)S(1)} %collective-permute-done.1.right, ...), custom_call_target="tpu_custom_call" | custom-call | flops 6710886400 | bytes 52428800 | tf_op jit(solution)/shard_map/pallas_call | solution.py:158
  92.8 0.0 copy-start
  92.8 0.0 copy-start.1
  92.8 3.0 %collective-permute-start.6 = (f32[256,256]{1,0:T(8,128)S(1)}, f32[256,256]{1,0:T(8,128)S(1)}, u32[]{:S(2)}, u32[]{:S(2)}) collective-permute-start(f32[256,256]{1,0:T(8,128)S(1)} %shard_map.79.own), channel_id=1, source_target_pairs={{0,1},{1,0},{2,3},{3,2},{4,5},{5,4},{6,7},{7,6},{8,9},{9,8},{10,11... | collective-permute-start | bytes 786440 | tf_op jit(solution)/shard_map/ppermute | solution.py:166
  95.9 1.8 %collective-permute-done.3.right = bf16[16,80,256]{2,1,0:T(8,128)(2,1)S(1)} collective-permute-done((bf16[16,80,256]{2,1,0:T(8,128)(2,1)S(1)}, bf16[16,80,256]{2,1,0:T(8,128)(2,1)S(1)}, u32[]{:S(2)}, u32[]{:S(2)}) %collective-permute-start.3) | collective-permute-done | bytes 655392 | tf_op jit(solution)/shard_map/ppermute | solution.py:119
  97.7 1.2 %shard_map.78.near = f32[256,256]{1,0:T(8,128)S(1)} custom-call(s32[2]{0:T(128)S(1)} %pad_add_fusion.where, bf16[4,2,2,16,5120]{4,3,2,1,0:T(8,128)(2,1)S(1)} %shard_map.77.held, bf16[16,80,256]{2,1,0:T(8,128)(2,1)S(1)} %slice.11.own, bf16[16,80,256]{2,1,0:T(8,128)(2,1)S(1)} %collective-permute-done.3.right, bf16[16,80,256]{2,1,0:T(8,128)(2,1)S(1)} %collective-permute-done.left), custom_call_target="tpu_custom_call" | custom-call | flops 5033164800 | bytes 39321600 | tf_op jit(solution)/shard_map/pallas_call | solution.py:167
  98.9 2.2 %collective-permute-done.6.partner = f32[256,256]{1,0:T(8,128)S(1)} collective-permute-done((f32[256,256]{1,0:T(8,128)S(1)}, f32[256,256]{1,0:T(8,128)S(1)}, u32[]{:S(2)}, u32[]{:S(2)}) %collective-permute-start.6) | collective-permute-done | bytes 262176 | tf_op jit(solution)/shard_map/ppermute | solution.py:166
  101.1 0.0 collective-permute-done.2.far
  101.1 0.0 copy-done
  101.1 0.0 copy-done.1
  101.1 2.7 %shard_map.80 = (bf16[256,256]{1,0:T(8,128)(2,1)}, bf16[256,256]{1,0:T(8,128)(2,1)}) custom-call(s32[2]{0:T(128)S(1)} %pad_add_fusion.where, bf16[4,2,2,16,5120]{4,3,2,1,0:T(8,128)(2,1)S(1)} %shard_map.77.held, bf16[16,80,256]{2,1,0:T(8,128)(2,1)S(1)} %collective-permute-done.2.far, f32[256,256]{1,0:T(8,128)S(1)} %shard_map.78.near, ...), custom_call_target="tpu_custom_call" | custom-call | flops 1677721600 | bytes 13107200 | tf_op jit(solution)/shard_map/pallas_call | solution.py:174
  (3 shorter events, 0.0 us)
Async XLA Ops:
  7.2 58.2 %copy-start.3 = (s32[1,256]{1,0:T(1,128)S(1)}, s32[1,256]{1,0:T(1,128)}, u32[]{:S(2)}) copy-start(s32[1,256]{1,0:T(1,128)} %param.11) | copy-start | bytes 3076
  7.2 76.7 %all-gather.3.cloned.1.call-start = ((), (), s32[]{:S(2)}) async-start(), calls=%async_computation | async-start | bytes 2949120 | tf_op jit(solution)/shard_map/all_gather | solution.py:101
  59.7 6.7 %copy-start.2 = (bf16[1920,256]{1,0:T(8,128)(2,1)}, bf16[1920,256]{1,0:T(8,128)(2,1)S(1)}, u32[]{:S(2)}) copy-start(bf16[1920,256]{1,0:T(8,128)(2,1)S(1)} %all-gather) | copy-start | bytes 2949124
  60.6 25.0 %collective-permute-start = (bf16[16,80,256]{2,1,0:T(8,128)(2,1)}, bf16[16,80,256]{2,1,0:T(8,128)(2,1)S(1)}, u32[]{:S(2)}, u32[]{:S(2)}) collective-permute-start(bf16[16,80,256]{2,1,0:T(8,128)(2,1)} %slice.12), channel_id=1, source_target_pairs={{0,768},{256,0},{512,256},{768,512},{1,769},{257,1},{513,257},{769... | collective-permute-start | bytes 1966088 | tf_op jit(solution)/shard_map/ppermute | solution.py:122
  66.4 12.0 %collective-permute-start.1 = (bf16[16,40,256]{2,1,0:T(8,128)(2,1)S(1)}, bf16[16,40,256]{2,1,0:T(8,128)(2,1)S(1)}, u32[]{:S(2)}, u32[]{:S(2)}) collective-permute-start(bf16[16,40,256]{2,1,0:T(8,128)(2,1)S(1)} %slice.10.own), channel_id=1, source_target_pairs={{0,256},{256,512},{512,768},{768,0},{1,257},{257,513},{513,769},{7... | collective-permute-start | bytes 983048 | tf_op jit(solution)/shard_map/ppermute | solution.py:119
  68.4 22.0 %collective-permute-start.4 = (bf16[16,40,256]{2,1,0:T(8,128)(2,1)S(1)}, bf16[16,40,256]{2,1,0:T(8,128)(2,1)S(1)}, u32[]{:S(2)}, u32[]{:S(2)}) collective-permute-start(bf16[16,40,256]{2,1,0:T(8,128)(2,1)S(1)} %slice.10.own), channel_id=1, source_target_pairs={{0,768},{256,0},{512,256},{768,512},{1,769},{257,1},{513,257},{769... | collective-permute-start | bytes 983048 | tf_op jit(solution)/shard_map/ppermute | solution.py:122
  78.5 12.3 %collective-permute-start.5 = (bf16[16,40,256]{2,1,0:T(8,128)(2,1)S(1)}, bf16[16,40,256]{2,1,0:T(8,128)(2,1)}, u32[]{:S(2)}, u32[]{:S(2)}) collective-permute-start(bf16[16,40,256]{2,1,0:T(8,128)(2,1)S(1)} %collective-permute-done.1.right), channel_id=1, source_target_pairs={{0,256},{256,512},{512,768},{768,0},{1,257},{257,513},{513,769},{7... | collective-permute-start | bytes 983048 | tf_op jit(solution)/shard_map/ppermute | solution.py:119
  81.5 16.1 %collective-permute-start.3 = (bf16[16,80,256]{2,1,0:T(8,128)(2,1)S(1)}, bf16[16,80,256]{2,1,0:T(8,128)(2,1)S(1)}, u32[]{:S(2)}, u32[]{:S(2)}) collective-permute-start(bf16[16,80,256]{2,1,0:T(8,128)(2,1)S(1)} %slice.11.own), channel_id=1, source_target_pairs={{0,256},{256,512},{512,768},{768,0},{1,257},{257,513},{513,769},{7... | collective-permute-start | bytes 1966088 | tf_op jit(solution)/shard_map/ppermute | solution.py:119
  85.7 15.4 %collective-permute-start.2 = (bf16[16,80,256]{2,1,0:T(8,128)(2,1)S(1)}, bf16[16,80,256]{2,1,0:T(8,128)(2,1)S(1)}, u32[]{:S(2)}, u32[]{:S(2)}) collective-permute-start(bf16[16,80,256]{2,1,0:T(8,128)(2,1)S(1)} %collective-permute-done.left), channel_id=1, source_target_pairs={{0,768},{256,0},{512,256},{768,512},{1,769},{257,1},{513,257},{769... | collective-permute-start | bytes 1966088 | tf_op jit(solution)/shard_map/ppermute | solution.py:122
  92.8 8.3 %copy-start = (f32[128]{0:T(128)S(1)}, f32[128]{0:T(128)}, u32[]{:S(2)}) copy-start(f32[128]{0:T(128)} %param.9) | copy-start | bytes 1540
  92.8 8.3 %copy-start.1 = (f32[128]{0:T(128)S(1)}, f32[128]{0:T(128)}, u32[]{:S(2)}) copy-start(f32[128]{0:T(128)} %param.10) | copy-start | bytes 1540
  92.8 8.3 %collective-permute-start.6 = (f32[256,256]{1,0:T(8,128)S(1)}, f32[256,256]{1,0:T(8,128)S(1)}, u32[]{:S(2)}, u32[]{:S(2)}) collective-permute-start(f32[256,256]{1,0:T(8,128)S(1)} %shard_map.79.own), channel_id=1, source_target_pairs={{0,1},{1,0},{2,3},{3,2},{4,5},{5,4},{6,7},{7,6},{8,9},{9,8},{10,11... | collective-permute-start | bytes 786440 | tf_op jit(solution)/shard_map/ppermute | solution.py:166
Sparse Core Ops, SparseCore 0:
  11.0 55.6 all-gather.2

commit v2 on v1

--- a/solution.py
+++ b/solution.py
@@ -66,14 +66,14 @@
     out[...] = sum(meet(where, held, n, weight[n]) for n in range(N_X))
 
 
-def query_kernel(where, held, own, right, left, out):
-    out[...] = (
-        meet(where, held, 0, own[...]) + meet(where, held, N_X - 1, right[...]) + meet(where, held, 1, left[...])
-    )
-
-
-def attend_kernel(head_size, where, held, far, near, own, partner, q_gain, k_gain, cosine, sine, bias, out, cache):
-    query = near[...] + meet(where, held, 2, far[...])
+def query_kernel(where, held, own, left, out):
+    out[...] = meet(where, held, 0, own[...]) + meet(where, held, 1, left[...])
+
+
+def attend_kernel(
+    head_size, where, held, far, right, near, own, partner, q_gain, k_gain, cosine, sine, bias, out, cache
+):
+    query = near[...] + meet(where, held, N_X - 1, right[...]) + meet(where, held, 2, far[...])
     key_value = own[...] + partner[...]
     key_rot = norm_rotate(key_value[:, :head_size], k_gain[...], cosine[...], sine[...]).astype(jnp.bfloat16)
     value_b = key_value[:, head_size:].astype(jnp.bfloat16)
@@ -121,12 +121,11 @@
     def down(a):
         return lax.ppermute(a, "x", [(x, (x - 1) % N_X) for x in range(N_X)])
 
-    query_left = down(column[:, :q_rows])
-    column, where, cosine, sine, bias = lax.optimization_barrier((column, where, cosine, sine, bias))
-    key_own = column[:, q_rows:]
+    query_own, key_own = column[:, :q_rows], column[:, q_rows:]
+    query_left = down(query_own)
+    key_own, where, cosine, sine = lax.optimization_barrier((key_own, where, cosine, sine))
     key_right, key_left = up(key_own), down(key_own)
-    column, key_right = lax.optimization_barrier((column, key_right))
-    query_own = column[:, :q_rows]
+    key_right, query_own, bias = lax.optimization_barrier((key_right, query_own, bias))
     query_right = up(query_own)
     key_far = up(key_right)
     whole, key_right = lax.optimization_barrier((whole, key_right))
@@ -167,20 +166,20 @@
     near = pl.pallas_call(
         query_kernel,
         out_shape=jax.ShapeDtypeStruct((count_total, q_cols), jnp.float32),
-        in_specs=[smem, *[VMEM] * 4],
+        in_specs=[smem, *[VMEM] * 3],
         out_specs=VMEM,
-        **settings(N_X - 1),
-    )(where, held, query_own, query_right, query_left)
+        **settings(2),
+    )(where, held, query_own, query_left)
     attention, cache = pl.pallas_call(
         functools.partial(attend_kernel, head_size),
         out_shape=(
             jax.ShapeDtypeStruct((count_total, q_cols), jnp.bfloat16),
             jax.ShapeDtypeStruct((count_total, pair_width), jnp.bfloat16),
         ),
-        in_specs=[smem, *[VMEM] * 10],
+        in_specs=[smem, *[VMEM] * 11],
         out_specs=(VMEM, VMEM),
-        **settings(1),
-    )(where, held, query_far, near, partial, partner, q_gain[None], k_gain[None], cosine, sine, bias)
+        **settings(2),
+    )(where, held, query_far, query_right, near, partial, partner, q_gain[None], k_gain[None], cosine, sine, bias)
     return attention, cache[:, None, :]
 
 

time: 111 us -> 110 us (level)
  the two profiles are of different devices: /device:TPU:40 before, /device:TPU:8 now
where the time goes in v2:
time: 110 us
  blocking collectives  51.6 us (47%)
  starting transfers between devices  23.1 us (21%)
  between operations  14.2 us (13%)
  waiting for transfers between devices  11.3 us (10%)
  Pallas kernels  7.7 us (7%)
  other arithmetic  1.86 us (2%)
    all_gather x1, blocking collectives, body(): column = lax.all_gather(block, 'z', axis=0)  48 us
    ppermute x3, starting transfers between devices, down(): return lax.ppermute(a, 'x', [(x, (x - 1) % N_X) for x in range(N_X)])  14.5 us
    ppermute x3, waiting for transfers between devices, up(): return lax.ppermute(a, 'x', [(x, (x + 1) % N_X) for x in range(N_X)])  7.81 us
    ppermute x3, starting transfers between devices, up(): return lax.ppermute(a, 'x', [(x, (x + 1) % N_X) for x in range(N_X)])  6.19 us
    all_gather x1, blocking collectives, body(): pair = lax.all_gather(tokens, 'core', axis=0, tiled=True)  3.6 us
    ppermute x1, waiting for transfers between devices, body(): partner = lax.ppermute(partial, 'yl', [(0, 1), (1, 0)])  3.42 us
    pallas_call x1, Pallas kernels, body(): pl.pallas_call(functools.partial(attend_kernel, head_size), out_shape=(ja...  2.9 us
    ppermute x1, starting transfers between devices, body(): partner = lax.ppermute(partial, 'yl', [(0, 1), (1, 0)])  2.36 us
  transfers between devices with their start and end apart: 8, of which 4 were waited for; matrix products, arithmetic and copies ran while one was open for 2% of the time, Pallas kernels for 4%

profile of v2, /device:TPU:8, one launch (start us, length us, event | category | flops | bytes accessed | tf_op | source)
XLA Modules:
  0.0 109.8 jit_solution(14314802698386713109)
XLA Ops:
  7.2 0.0 copy-start.2
  7.2 0.0 all-gather.3.cloned.1.call-start
  7.2 3.6 %all_gather.14 = bf16[32,5120]{1,0:T(8,128)(2,1)} all-gather(bf16[16,5120]{1,0:T(8,128)(2,1)} %param.6), channel_id=1, replica_groups=mesh['x'=4,'z'=16,'yh'=4,'core'=2,'yl'=2] {'core'}, dimensions={0}, use_global_device_ids=true | all-gather | bytes 491520 | tf_op jit(solution)/shard_map/all_gather | solution.py:100
  10.8 0.0 all-gather.3.cloned.1.call-update
  10.8 0.8 pad_maximum_fusion.2
  11.6 48.0 %all-gather = bf16[1920,256]{1,0:T(8,128)(2,1)S(1)} all-gather(bf16[120,256]{1,0:T(8,128)(2,1)S(1)} %pad_maximum_fusion.2), channel_id=2, replica_groups=mesh['x'=4,'z'=16,'yh'=4,'core'=2,'yl'=2] {'z'}, dimensions={0}, use_global_device_ids=true | all-gather | bytes 1044480 | tf_op jit(solution)/shard_map/all_gather | solution.py:117
  59.7 4.7 %collective-permute-start = (bf16[16,80,256]{2,1,0:T(8,128)(2,1)S(1)}, bf16[16,80,256]{2,1,0:T(8,128)(2,1)S(1)}, u32[]{:S(2)}, u32[]{:S(2)}) collective-permute-start(bf16[16,80,256]{2,1,0:T(8,128)(2,1)S(1)} %slice.9.own), channel_id=1, source_target_pairs={{0,768},{256,0},{512,256},{768,512},{1,769},{257,1},{513,257},{769... | collective-permute-start | bytes 1966088 | tf_op jit(solution)/shard_map/ppermute | solution.py:122
  64.5 0.1 pad_add_fusion.where
  64.5 0.0 copy-done.2
  64.5 0.2 convert_reduce_fusion
  64.7 0.5 fusion.2
  65.3 0.1 pad_maximum_fusion
  65.4 1.9 %collective-permute-start.1 = (bf16[16,40,256]{2,1,0:T(8,128)(2,1)S(1)}, bf16[16,40,256]{2,1,0:T(8,128)(2,1)S(1)}, u32[]{:S(2)}, u32[]{:S(2)}) collective-permute-start(bf16[16,40,256]{2,1,0:T(8,128)(2,1)S(1)} %slice.8.own), channel_id=1, source_target_pairs={{0,256},{256,512},{512,768},{768,0},{1,257},{257,513},{513,769},{7... | collective-permute-start | bytes 983048 | tf_op jit(solution)/shard_map/ppermute | solution.py:119
  67.4 5.1 %collective-permute-start.4 = (bf16[16,40,256]{2,1,0:T(8,128)(2,1)S(1)}, bf16[16,40,256]{2,1,0:T(8,128)(2,1)S(1)}, u32[]{:S(2)}, u32[]{:S(2)}) collective-permute-start(bf16[16,40,256]{2,1,0:T(8,128)(2,1)S(1)} %slice.8.own), channel_id=1, source_target_pairs={{0,768},{256,0},{512,256},{768,512},{1,769},{257,1},{513,257},{769... | collective-permute-start | bytes 983048 | tf_op jit(solution)/shard_map/ppermute | solution.py:122
  72.5 0.1 fusion.1.bias
  72.6 4.9 %collective-permute-done.1.right = bf16[16,40,256]{2,1,0:T(8,128)(2,1)S(1)} collective-permute-done((bf16[16,40,256]{2,1,0:T(8,128)(2,1)S(1)}, bf16[16,40,256]{2,1,0:T(8,128)(2,1)S(1)}, u32[]{:S(2)}, u32[]{:S(2)}) %collective-permute-start.1) | collective-permute-done | bytes 327712 | tf_op jit(solution)/shard_map/ppermute | solution.py:119
  77.5 1.9 %collective-permute-start.5 = (bf16[16,40,256]{2,1,0:T(8,128)(2,1)S(1)}, bf16[16,40,256]{2,1,0:T(8,128)(2,1)}, u32[]{:S(2)}, u32[]{:S(2)}) collective-permute-start(bf16[16,40,256]{2,1,0:T(8,128)(2,1)S(1)} %collective-permute-done.1.right), channel_id=1, source_target_pairs={{0,256},{256,512},{512,768},{768,0},{1,257},{257,513},{513,769},{7... | collective-permute-start | bytes 983048 | tf_op jit(solution)/shard_map/ppermute | solution.py:119
  79.4 2.4 %collective-permute-start.3 = (bf16[16,80,256]{2,1,0:T(8,128)(2,1)S(1)}, bf16[16,80,256]{2,1,0:T(8,128)(2,1)S(1)}, u32[]{:S(2)}, u32[]{:S(2)}) collective-permute-start(bf16[16,80,256]{2,1,0:T(8,128)(2,1)S(1)} %slice.9.own), channel_id=1, source_target_pairs={{0,256},{256,512},{512,768},{768,0},{1,257},{257,513},{513,769},{7... | collective-permute-start | bytes 1966088 | tf_op jit(solution)/shard_map/ppermute | solution.py:119
  81.8 0.0 all-gather.3.cloned.1.call-done
  81.8 1.7 %shard_map.77.held = bf16[4,2,2,16,5120]{4,3,2,1,0:T(8,128)(2,1)S(1)} custom-call(bf16[4,2,2,16,5120]{4,3,2,1,0:T(8,128)(2,1)} %bitcast.13), custom_call_target="tpu_custom_call" | custom-call | bytes 52428800 | tf_op jit(solution)/shard_map/pallas_call | solution.py:133
  83.5 0.0 collective-permute-done.left
  83.5 4.7 %collective-permute-start.2 = (bf16[16,80,256]{2,1,0:T(8,128)(2,1)S(1)}, bf16[16,80,256]{2,1,0:T(8,128)(2,1)S(1)}, u32[]{:S(2)}, u32[]{:S(2)}) collective-permute-start(bf16[16,80,256]{2,1,0:T(8,128)(2,1)S(1)} %collective-permute-done.left), channel_id=1, source_target_pairs={{0,768},{256,0},{512,256},{768,512},{1,769},{257,1},{513,257},{769... | collective-permute-start | bytes 1966088 | tf_op jit(solution)/shard_map/ppermute | solution.py:122
  88.2 0.0 collective-permute-done.4.left
  88.2 1.5 %collective-permute-done.5.far = bf16[16,40,256]{2,1,0:T(8,128)(2,1)} collective-permute-done((bf16[16,40,256]{2,1,0:T(8,128)(2,1)S(1)}, bf16[16,40,256]{2,1,0:T(8,128)(2,1)}, u32[]{:S(2)}, u32[]{:S(2)}) %collective-permute-start.5) | collective-permute-done | bytes 327712 | tf_op jit(solution)/shard_map/ppermute | solution.py:119
  89.8 2.0 %shard_map.79.own = f32[256,256]{1,0:T(8,128)S(1)} custom-call(s32[2]{0:T(128)S(1)} %pad_add_fusion.where, bf16[4,2,2,16,5120]{4,3,2,1,0:T(8,128)(2,1)S(1)} %shard_map.77.held, bf16[16,40,256]{2,1,0:T(8,128)(2,1)S(1)} %slice.8.own, bf16[16,40,256]{2,1,0:T(8,128)(2,1)S(1)} %collective-permute-done.1.right, ...), custom_call_target="tpu_custom_call" | custom-call | flops 6710886400 | bytes 52428800 | tf_op jit(solution)/shard_map/pallas_call | solution.py:157
  91.8 0.0 copy-start
  91.8 0.0 copy-start.1
  91.8 2.4 %collective-permute-start.6 = (f32[256,256]{1,0:T(8,128)S(1)}, f32[256,256]{1,0:T(8,128)S(1)}, u32[]{:S(2)}, u32[]{:S(2)}) collective-permute-start(f32[256,256]{1,0:T(8,128)S(1)} %shard_map.79.own), channel_id=1, source_target_pairs={{0,1},{1,0},{2,3},{3,2},{4,5},{5,4},{6,7},{7,6},{8,9},{9,8},{10,11... | collective-permute-start | bytes 786440 | tf_op jit(solution)/shard_map/ppermute | solution.py:165
  94.2 1.1 shard_map.78.near
  95.3 1.4 %collective-permute-done.3.right = bf16[16,80,256]{2,1,0:T(8,128)(2,1)S(1)} collective-permute-done((bf16[16,80,256]{2,1,0:T(8,128)(2,1)S(1)}, bf16[16,80,256]{2,1,0:T(8,128)(2,1)S(1)}, u32[]{:S(2)}, u32[]{:S(2)}) %collective-permute-start.3) | collective-permute-done | bytes 655392 | tf_op jit(solution)/shard_map/ppermute | solution.py:119
  96.7 3.4 %collective-permute-done.6.partner = f32[256,256]{1,0:T(8,128)S(1)} collective-permute-done((f32[256,256]{1,0:T(8,128)S(1)}, f32[256,256]{1,0:T(8,128)S(1)}, u32[]{:S(2)}, u32[]{:S(2)}) %collective-permute-start.6) | collective-permute-done | bytes 262176 | tf_op jit(solution)/shard_map/ppermute | solution.py:165
  100.1 0.0 collective-permute-done.2.far
  100.1 0.0 copy-done
  100.1 0.0 copy-done.1
  100.1 2.9 %shard_map.80 = (bf16[256,256]{1,0:T(8,128)(2,1)}, bf16[256,256]{1,0:T(8,128)(2,1)}) custom-call(s32[2]{0:T(128)S(1)} %pad_add_fusion.where, bf16[4,2,2,16,5120]{4,3,2,1,0:T(8,128)(2,1)S(1)} %shard_map.77.held, bf16[16,80,256]{2,1,0:T(8,128)(2,1)S(1)} %collective-permute-done.2.far, bf16[16,80,256]{2,1,0:T(8,128)(2,1)S(1)} %collective-permute-done.3.right, ...), custom_call_target="tpu_custom_call" | custom-call | flops 3355443200 | bytes 26214400 | tf_op jit(solution)/shard_map/pallas_call | solution.py:173
  (4 shorter events, 0.1 us)
Async XLA Ops:
  7.2 57.4 %copy-start.2 = (s32[1,256]{1,0:T(1,128)S(1)}, s32[1,256]{1,0:T(1,128)}, u32[]{:S(2)}) copy-start(s32[1,256]{1,0:T(1,128)} %param.11) | copy-start | bytes 3076
  7.2 74.6 %all-gather.3.cloned.1.call-start = ((), (), s32[]{:S(2)}) async-start(), calls=%async_computation | async-start | bytes 2949120 | tf_op jit(solution)/shard_map/all_gather | solution.py:101
  59.7 23.8 %collective-permute-start = (bf16[16,80,256]{2,1,0:T(8,128)(2,1)S(1)}, bf16[16,80,256]{2,1,0:T(8,128)(2,1)S(1)}, u32[]{:S(2)}, u32[]{:S(2)}) collective-permute-start(bf16[16,80,256]{2,1,0:T(8,128)(2,1)S(1)} %slice.9.own), channel_id=1, source_target_pairs={{0,768},{256,0},{512,256},{768,512},{1,769},{257,1},{513,257},{769... | collective-permute-start | bytes 1966088 | tf_op jit(solution)/shard_map/ppermute | solution.py:122
  65.4 12.0 %collective-permute-start.1 = (bf16[16,40,256]{2,1,0:T(8,128)(2,1)S(1)}, bf16[16,40,256]{2,1,0:T(8,128)(2,1)S(1)}, u32[]{:S(2)}, u32[]{:S(2)}) collective-permute-start(bf16[16,40,256]{2,1,0:T(8,128)(2,1)S(1)} %slice.8.own), channel_id=1, source_target_pairs={{0,256},{256,512},{512,768},{768,0},{1,257},{257,513},{513,769},{7... | collective-permute-start | bytes 983048 | tf_op jit(solution)/shard_map/ppermute | solution.py:119
  67.4 20.9 %collective-permute-start.4 = (bf16[16,40,256]{2,1,0:T(8,128)(2,1)S(1)}, bf16[16,40,256]{2,1,0:T(8,128)(2,1)S(1)}, u32[]{:S(2)}, u32[]{:S(2)}) collective-permute-start(bf16[16,40,256]{2,1,0:T(8,128)(2,1)S(1)} %slice.8.own), channel_id=1, source_target_pairs={{0,768},{256,0},{512,256},{768,512},{1,769},{257,1},{513,257},{769... | collective-permute-start | bytes 983048 | tf_op jit(solution)/shard_map/ppermute | solution.py:122
  77.5 12.3 %collective-permute-start.5 = (bf16[16,40,256]{2,1,0:T(8,128)(2,1)S(1)}, bf16[16,40,256]{2,1,0:T(8,128)(2,1)}, u32[]{:S(2)}, u32[]{:S(2)}) collective-permute-start(bf16[16,40,256]{2,1,0:T(8,128)(2,1)S(1)} %collective-permute-done.1.right), channel_id=1, source_target_pairs={{0,256},{256,512},{512,768},{768,0},{1,257},{257,513},{513,769},{7... | collective-permute-start | bytes 983048 | tf_op jit(solution)/shard_map/ppermute | solution.py:119
  79.4 17.3 %collective-permute-start.3 = (bf16[16,80,256]{2,1,0:T(8,128)(2,1)S(1)}, bf16[16,80,256]{2,1,0:T(8,128)(2,1)S(1)}, u32[]{:S(2)}, u32[]{:S(2)}) collective-permute-start(bf16[16,80,256]{2,1,0:T(8,128)(2,1)S(1)} %slice.9.own), channel_id=1, source_target_pairs={{0,256},{256,512},{512,768},{768,0},{1,257},{257,513},{513,769},{7... | collective-permute-start | bytes 1966088 | tf_op jit(solution)/shard_map/ppermute | solution.py:119
  83.5 16.6 %collective-permute-start.2 = (bf16[16,80,256]{2,1,0:T(8,128)(2,1)S(1)}, bf16[16,80,256]{2,1,0:T(8,128)(2,1)S(1)}, u32[]{:S(2)}, u32[]{:S(2)}) collective-permute-start(bf16[16,80,256]{2,1,0:T(8,128)(2,1)S(1)} %collective-permute-done.left), channel_id=1, source_target_pairs={{0,768},{256,0},{512,256},{768,512},{1,769},{257,1},{513,257},{769... | collective-permute-start | bytes 1966088 | tf_op jit(solution)/shard_map/ppermute | solution.py:122
  91.8 8.3 %copy-start = (f32[128]{0:T(128)S(1)}, f32[128]{0:T(128)}, u32[]{:S(2)}) copy-start(f32[128]{0:T(128)} %param.9) | copy-start | bytes 1540
  91.8 8.3 %copy-start.1 = (f32[128]{0:T(128)S(1)}, f32[128]{0:T(128)}, u32[]{:S(2)}) copy-start(f32[128]{0:T(128)} %param.10) | copy-start | bytes 1540
  91.8 8.3 %collective-permute-start.6 = (f32[256,256]{1,0:T(8,128)S(1)}, f32[256,256]{1,0:T(8,128)S(1)}, u32[]{:S(2)}, u32[]{:S(2)}) collective-permute-start(f32[256,256]{1,0:T(8,128)S(1)} %shard_map.79.own), channel_id=1, source_target_pairs={{0,1},{1,0},{2,3},{3,2},{4,5},{5,4},{6,7},{7,6},{8,9},{9,8},{10,11... | collective-permute-start | bytes 786440 | tf_op jit(solution)/shard_map/ppermute | solution.py:165
Sparse Core Ops, SparseCore 0:
  11.0 57.7 all-gather.2

commit v3 on v2

--- a/solution.py
+++ b/solution.py
@@ -40,11 +40,10 @@
     )
 
 
-def order_kernel(whole, held, sems):
+def order_kernel(where, mine, other, held, sems):
     copies = [
-        pltpu.make_async_copy(whole.at[:, near, core], held.at[:, core, near], sems.at[core, near])
-        for core in range(N_CORE)
-        for near in range(N_YL)
+        pltpu.make_async_copy(rows, held.at[:, core], sems.at[n])
+        for n, (rows, core) in enumerate(((mine, where[2]), (other, 1 - where[2])))
     ]
     for copy in copies:
         copy.start()
@@ -95,10 +94,11 @@
     q_rows, q_cols = w_query.shape
     kv_rows, _, pair_width = keyval_weight.shape
     head_size = pair_width // 2
-    where = jnp.stack([lax.axis_index(axis) for axis in ("x", "yl")]).astype(jnp.int32)
-
-    pair = lax.all_gather(tokens, "core", axis=0, tiled=True)
-    whole = lax.all_gather(pair, ("yh", "yl"), axis=0, tiled=True)
+    where = jnp.stack([lax.axis_index(axis) for axis in ("x", "yl", "core")]).astype(jnp.int32)
+
+    mine = lax.all_to_all(
+        jnp.broadcast_to(tokens[None], (N_YH * N_YL, *tokens.shape)), ("yh", "yl"), split_axis=0, concat_axis=0
+    )
 
     seg_ids = segments.reshape(-1)
     count_total = seg_ids.shape[0]
@@ -128,21 +128,23 @@
     key_right, query_own, bias = lax.optimization_barrier((key_right, query_own, bias))
     query_right = up(query_own)
     key_far = up(key_right)
-    whole, key_right = lax.optimization_barrier((whole, key_right))
+    other = lax.ppermute(mine, "core", [(0, 1), (1, 0)])
     depth = N_X * N_Z * q_rows
+    mine, other = (
+        a.reshape(N_YH, N_YL, tokens.shape[0], depth) for a in (mine, other)
+    )
+    smem = pl.BlockSpec(memory_space=pltpu.SMEM)
     held = pl.pallas_call(
         order_kernel,
         out_shape=jax.ShapeDtypeStruct((N_YH, N_CORE, N_YL, tokens.shape[0], depth), jnp.bfloat16),
-        in_specs=[HBM],
+        in_specs=[smem, VMEM, VMEM],
         out_specs=VMEM,
-        scratch_shapes=[pltpu.SemaphoreType.DMA((N_CORE, N_YL))],
+        scratch_shapes=[pltpu.SemaphoreType.DMA((N_CORE,))],
         cost_estimate=pl.CostEstimate(flops=0, bytes_accessed=10 * 4 * count_total * depth, transcendentals=0),
         compiler_params=pltpu.CompilerParams(vmem_limit_bytes=16 << 20),
-    )(pltpu.with_memory_space_constraint(whole.reshape(N_YH, N_YL, N_CORE, tokens.shape[0], depth), pltpu.HBM))
-
+    )(where, mine, other)
     query_left, held = lax.optimization_barrier((query_left, held))
     query_far = down(query_left)
-    smem = pl.BlockSpec(memory_space=pltpu.SMEM)
 
     def settings(slots):
         return dict(

time: 110 us -> 111 us (level)
  the two profiles are of different devices: /device:TPU:8 before, /device:TPU:1 now
where the time goes in v3:
time: 111 us; the launch traced here: 110 us
  blocking collectives  42.5 us (38%)
  starting transfers between devices  39.6 us (36%)
  waiting for transfers between devices  15.7 us (14%)
  Pallas kernels  6.31 us (6%)
  local copies, waits for them, and re-layouts  4.12 us (4%)
    all_gather x1, blocking collectives, body(): column = lax.all_gather(block, 'z', axis=0)  42.5 us
    ppermute x3, waiting for transfers between devices, up(): return lax.ppermute(a, 'x', [(x, (x + 1) % N_X) for x in range(N_X)])  15.6 us
    ppermute x3, starting transfers between devices, down(): return lax.ppermute(a, 'x', [(x, (x - 1) % N_X) for x in range(N_X)])  13.3 us
    ppermute x1, starting transfers between devices, body(): other = lax.ppermute(mine, 'core', [(0, 1), (1, 0)])  8.95 us
    all_to_all x1, starting transfers between devices, body(): lax.all_to_all(jnp.broadcast_to(tokens[None], (N_YH * N_YL, *tokens.shape...  7.78 us
    ppermute x3, starting transfers between devices, up(): return lax.ppermute(a, 'x', [(x, (x + 1) % N_X) for x in range(N_X)])  5.75 us
    ppermute x1, starting transfers between devices, body(): partner = lax.ppermute(partial, 'yl', [(0, 1), (1, 0)])  3.83 us
    pallas_call x1, Pallas kernels, body(): pl.pallas_call(functools.partial(attend_kernel, head_size), out_shape=(ja...  2.9 us
  transfers between devices with their start and end apart: 9, of which 3 were waited for; matrix products, arithmetic and copies ran while one was open for 2% of the time, Pallas kernels for 3%

profile of v3, /device:TPU:1, one launch (start us, length us, event | category | flops | bytes accessed | tf_op | source)
XLA Modules:
  0.0 110.1 jit_solution(14006908444570120094)
XLA Ops:
  0.6 2.1 %broadcast_in_dim.27 = bf16[8,16,5120]{2,1,0:T(8,128)(2,1)} broadcast(bf16[16,5120]{1,0:T(8,128)(2,1)} %param.6), dimensions={1,2} | broadcast | bytes 1474560 | tf_op jit(solution)/shard_map/broadcast_in_dim | solution.py:100
  2.7 0.0 copy-start.3
  2.7 0.0 copy-start.4
  2.7 7.8 %all-to-all-start = ((bf16[8,16,5120]{2,1,0:T(8,128)(2,1)}), bf16[8,16,5120]{2,1,0:T(8,128)(2,1)S(1)}, u32[]{:S(2)}, u32[]{:S(2)}) async-start(bf16[8,16,5120]{2,1,0:T(8,128)(2,1)} %broadcast_in_dim.27), calls=%async_computation | async-start | bytes 2621440 | tf_op jit(solution)/shard_map/all_to_all | solution.py:99
  10.5 0.0 copy-done.3
  10.5 0.0 copy-done.4
  10.6 0.0 copy-start.5
  10.6 42.5 %all-gather = bf16[1920,256]{1,0:T(8,128)(2,1)S(1)} all-gather(bf16[120,256]{1,0:T(8,128)(2,1)S(1)} %pad_maximum_fusion.2), channel_id=2, replica_groups=mesh['x'=4,'z'=16,'yh'=4,'core'=2,'yl'=2] {'z'}, dimensions={0}, use_global_device_ids=true | all-gather | bytes 1044480 | tf_op jit(solution)/shard_map/all_gather | solution.py:117
  53.0 0.0 copy-start.2
  53.0 0.9 copy-done.2
  54.0 4.1 %collective-permute-start = (bf16[16,80,256]{2,1,0:T(8,128)(2,1)S(1)}, bf16[16,80,256]{2,1,0:T(8,128)(2,1)S(1)}, u32[]{:S(2)}, u32[]{:S(2)}) collective-permute-start(bf16[16,80,256]{2,1,0:T(8,128)(2,1)S(1)} %slice.9.own), channel_id=1, source_target_pairs={{0,768},{256,0},{512,256},{768,512},{1,769},{257,1},{513,257},{769... | collective-permute-start | bytes 1966088 | tf_op jit(solution)/shard_map/ppermute | solution.py:122
  58.2 1.0 slice.8.own
  59.2 0.0 copy-done.5
  59.2 0.2 convert_reduce_fusion
  59.4 0.0 all-to-all-done
  59.4 8.9 %collective-permute-start.1 = (bf16[8,16,5120]{2,1,0:T(8,128)(2,1)S(1)}, bf16[8,16,5120]{2,1,0:T(8,128)(2,1)S(1)}, u32[]{:S(2)}, u32[]{:S(2)}) collective-permute-start(bf16[8,16,5120]{2,1,0:T(8,128)(2,1)S(1)} %all-to-all-done), channel_id=1, source_target_pairs={{0,2},{2,0},{1,3},{3,1},{4,6},{6,4},{5,7},{7,5},{8,10},{10,8},{9,1... | collective-permute-start | bytes 3932168 | tf_op jit(solution)/shard_map/ppermute | solution.py:131
  68.3 0.1 pad_add_fusion.where
  68.4 0.5 fusion.2
  69.0 0.1 pad_maximum_fusion
  69.1 1.9 %collective-permute-start.3 = (bf16[16,40,256]{2,1,0:T(8,128)(2,1)S(1)}, bf16[16,40,256]{2,1,0:T(8,128)(2,1)S(1)}, u32[]{:S(2)}, u32[]{:S(2)}) collective-permute-start(bf16[16,40,256]{2,1,0:T(8,128)(2,1)S(1)} %slice.8.own), channel_id=1, source_target_pairs={{0,256},{256,512},{512,768},{768,0},{1,257},{257,513},{513,769},{7... | collective-permute-start | bytes 983048 | tf_op jit(solution)/shard_map/ppermute | solution.py:119
  71.0 4.6 %collective-permute-start.5 = (bf16[16,40,256]{2,1,0:T(8,128)(2,1)S(1)}, bf16[16,40,256]{2,1,0:T(8,128)(2,1)S(1)}, u32[]{:S(2)}, u32[]{:S(2)}) collective-permute-start(bf16[16,40,256]{2,1,0:T(8,128)(2,1)S(1)} %slice.8.own), channel_id=1, source_target_pairs={{0,768},{256,0},{512,256},{768,512},{1,769},{257,1},{513,257},{769... | collective-permute-start | bytes 983048 | tf_op jit(solution)/shard_map/ppermute | solution.py:122
  75.6 0.1 fusion.1.bias
  75.7 5.8 %collective-permute-done.3.right = bf16[16,40,256]{2,1,0:T(8,128)(2,1)S(1)} collective-permute-done((bf16[16,40,256]{2,1,0:T(8,128)(2,1)S(1)}, bf16[16,40,256]{2,1,0:T(8,128)(2,1)S(1)}, u32[]{:S(2)}, u32[]{:S(2)}) %collective-permute-start.3) | collective-permute-done | bytes 327712 | tf_op jit(solution)/shard_map/ppermute | solution.py:119
  81.6 1.9 %collective-permute-start.6 = (bf16[16,40,256]{2,1,0:T(8,128)(2,1)S(1)}, bf16[16,40,256]{2,1,0:T(8,128)(2,1)S(1)}, u32[]{:S(2)}, u32[]{:S(2)}) collective-permute-start(bf16[16,40,256]{2,1,0:T(8,128)(2,1)S(1)} %collective-permute-done.3.right), channel_id=1, source_target_pairs={{0,256},{256,512},{512,768},{768,0},{1,257},{257,513},{513,769},{7... | collective-permute-start | bytes 983048 | tf_op jit(solution)/shard_map/ppermute | solution.py:119
  83.5 1.9 %collective-permute-start.4 = (bf16[16,80,256]{2,1,0:T(8,128)(2,1)S(1)}, bf16[16,80,256]{2,1,0:T(8,128)(2,1)S(1)}, u32[]{:S(2)}, u32[]{:S(2)}) collective-permute-start(bf16[16,80,256]{2,1,0:T(8,128)(2,1)S(1)} %slice.9.own), channel_id=1, source_target_pairs={{0,256},{256,512},{512,768},{768,0},{1,257},{257,513},{513,769},{7... | collective-permute-start | bytes 1966088 | tf_op jit(solution)/shard_map/ppermute | solution.py:119
  85.4 0.0 collective-permute-done.1
  85.4 0.7 shard_map.77.held
  86.2 0.0 collective-permute-done.left
  86.2 4.6 %collective-permute-start.2 = (bf16[16,80,256]{2,1,0:T(8,128)(2,1)S(1)}, bf16[16,80,256]{2,1,0:T(8,128)(2,1)S(1)}, u32[]{:S(2)}, u32[]{:S(2)}) collective-permute-start(bf16[16,80,256]{2,1,0:T(8,128)(2,1)S(1)} %collective-permute-done.left), channel_id=1, source_target_pairs={{0,768},{256,0},{512,256},{768,512},{1,769},{257,1},{513,257},{769... | collective-permute-start | bytes 1966088 | tf_op jit(solution)/shard_map/ppermute | solution.py:122
  90.8 0.0 collective-permute-done.5.left
  90.8 2.3 %collective-permute-done.6.far = bf16[16,40,256]{2,1,0:T(8,128)(2,1)S(1)} collective-permute-done((bf16[16,40,256]{2,1,0:T(8,128)(2,1)S(1)}, bf16[16,40,256]{2,1,0:T(8,128)(2,1)S(1)}, u32[]{:S(2)}, u32[]{:S(2)}) %collective-permute-start.6) | collective-permute-done | bytes 327712 | tf_op jit(solution)/shard_map/ppermute | solution.py:119
  93.1 1.6 %shard_map.79.own = f32[256,256]{1,0:T(8,128)S(1)} custom-call(s32[3]{0:T(128)S(1)} %pad_add_fusion.where, bf16[4,2,2,16,5120]{4,3,2,1,0:T(8,128)(2,1)S(1)} %shard_map.77.held, bf16[16,40,256]{2,1,0:T(8,128)(2,1)S(1)} %slice.8.own, bf16[16,40,256]{2,1,0:T(8,128)(2,1)S(1)} %collective-permute-done.3.right, ...), custom_call_target="tpu_custom_call" | custom-call | flops 6710886400 | bytes 52428800 | tf_op jit(solution)/shard_map/pallas_call | solution.py:159
  94.7 0.0 copy-start
  94.7 0.0 copy-start.1
  94.7 3.8 %collective-permute-start.7 = (f32[256,256]{1,0:T(8,128)S(1)}, f32[256,256]{1,0:T(8,128)S(1)}, u32[]{:S(2)}, u32[]{:S(2)}) collective-permute-start(f32[256,256]{1,0:T(8,128)S(1)} %shard_map.79.own), channel_id=1, source_target_pairs={{0,1},{1,0},{2,3},{3,2},{4,5},{5,4},{6,7},{7,6},{8,9},{9,8},{10,11... | collective-permute-start | bytes 786440 | tf_op jit(solution)/shard_map/ppermute | solution.py:167
  98.6 1.1 shard_map.78.near
  99.6 7.5 %collective-permute-done.4.right = bf16[16,80,256]{2,1,0:T(8,128)(2,1)S(1)} collective-permute-done((bf16[16,80,256]{2,1,0:T(8,128)(2,1)S(1)}, bf16[16,80,256]{2,1,0:T(8,128)(2,1)S(1)}, u32[]{:S(2)}, u32[]{:S(2)}) %collective-permute-start.4) | collective-permute-done | bytes 655392 | tf_op jit(solution)/shard_map/ppermute | solution.py:119
  107.1 0.0 collective-permute-done.7.partner
  107.1 0.0 collective-permute-done.2.far
  107.1 0.0 copy-done
  107.1 0.0 copy-done.1
  107.2 2.9 %shard_map.80 = (bf16[256,256]{1,0:T(8,128)(2,1)}, bf16[256,256]{1,0:T(8,128)(2,1)}) custom-call(s32[3]{0:T(128)S(1)} %pad_add_fusion.where, bf16[4,2,2,16,5120]{4,3,2,1,0:T(8,128)(2,1)S(1)} %shard_map.77.held, bf16[16,80,256]{2,1,0:T(8,128)(2,1)S(1)} %collective-permute-done.2.far, bf16[16,80,256]{2,1,0:T(8,128)(2,1)S(1)} %collective-permute-done.4.right, ...), custom_call_target="tpu_custom_call" | custom-call | flops 3355443200 | bytes 26214400 | tf_op jit(solution)/shard_map/pallas_call | solution.py:175
  (4 shorter events, 0.1 us)
Async XLA Ops:
  2.7 7.8 %copy-start.3 = (bf16[80,256]{1,0:T(8,128)(2,1)S(1)}, bf16[80,256]{1,0:T(8,128)(2,1)}, u32[]{:S(2)}) copy-start(bf16[80,256]{1,0:T(8,128)(2,1)} %param.7) | copy-start | bytes 122884
  2.7 7.8 %copy-start.4 = (bf16[40,1,256]{2,0,1:T(8,128)(2,1)S(1)}, bf16[40,1,256]{2,0,1:T(8,128)(2,1)}, u32[]{:S(2)}) copy-start(bf16[40,1,256]{2,0,1:T(8,128)(2,1)} %param.8) | copy-start | bytes 61444
  2.7 56.6 %all-to-all-start = ((bf16[8,16,5120]{2,1,0:T(8,128)(2,1)}), bf16[8,16,5120]{2,1,0:T(8,128)(2,1)S(1)}, u32[]{:S(2)}, u32[]{:S(2)}) async-start(bf16[8,16,5120]{2,1,0:T(8,128)(2,1)} %broadcast_in_dim.27), calls=%async_computation | async-start | bytes 2621440 | tf_op jit(solution)/shard_map/all_to_all | solution.py:99
  10.6 48.6 %copy-start.5 = (s32[1,256]{1,0:T(1,128)S(1)}, s32[1,256]{1,0:T(1,128)}, u32[]{:S(2)}) copy-start(s32[1,256]{1,0:T(1,128)} %param.11) | copy-start | bytes 3076
  53.0 0.9 copy-start.2
  54.0 32.1 %collective-permute-start = (bf16[16,80,256]{2,1,0:T(8,128)(2,1)S(1)}, bf16[16,80,256]{2,1,0:T(8,128)(2,1)S(1)}, u32[]{:S(2)}, u32[]{:S(2)}) collective-permute-start(bf16[16,80,256]{2,1,0:T(8,128)(2,1)S(1)} %slice.9.own), channel_id=1, source_target_pairs={{0,768},{256,0},{512,256},{768,512},{1,769},{257,1},{513,257},{769... | collective-permute-start | bytes 1966088 | tf_op jit(solution)/shard_map/ppermute | solution.py:122
  59.4 26.0 %collective-permute-start.1 = (bf16[8,16,5120]{2,1,0:T(8,128)(2,1)S(1)}, bf16[8,16,5120]{2,1,0:T(8,128)(2,1)S(1)}, u32[]{:S(2)}, u32[]{:S(2)}) collective-permute-start(bf16[8,16,5120]{2,1,0:T(8,128)(2,1)S(1)} %all-to-all-done), channel_id=1, source_target_pairs={{0,2},{2,0},{1,3},{3,1},{4,6},{6,4},{5,7},{7,5},{8,10},{10,8},{9,1... | collective-permute-start | bytes 3932168 | tf_op jit(solution)/shard_map/ppermute | solution.py:131
  69.1 12.4 %collective-permute-start.3 = (bf16[16,40,256]{2,1,0:T(8,128)(2,1)S(1)}, bf16[16,40,256]{2,1,0:T(8,128)(2,1)S(1)}, u32[]{:S(2)}, u32[]{:S(2)}) collective-permute-start(bf16[16,40,256]{2,1,0:T(8,128)(2,1)S(1)} %slice.8.own), channel_id=1, source_target_pairs={{0,256},{256,512},{512,768},{768,0},{1,257},{257,513},{513,769},{7... | collective-permute-start | bytes 983048 | tf_op jit(solution)/shard_map/ppermute | solution.py:119
  71.0 19.7 %collective-permute-start.5 = (bf16[16,40,256]{2,1,0:T(8,128)(2,1)S(1)}, bf16[16,40,256]{2,1,0:T(8,128)(2,1)S(1)}, u32[]{:S(2)}, u32[]{:S(2)}) collective-permute-start(bf16[16,40,256]{2,1,0:T(8,128)(2,1)S(1)} %slice.8.own), channel_id=1, source_target_pairs={{0,768},{256,0},{512,256},{768,512},{1,769},{257,1},{513,257},{769... | collective-permute-start | bytes 983048 | tf_op jit(solution)/shard_map/ppermute | solution.py:122
  81.6 11.5 %collective-permute-start.6 = (bf16[16,40,256]{2,1,0:T(8,128)(2,1)S(1)}, bf16[16,40,256]{2,1,0:T(8,128)(2,1)S(1)}, u32[]{:S(2)}, u32[]{:S(2)}) collective-permute-start(bf16[16,40,256]{2,1,0:T(8,128)(2,1)S(1)} %collective-permute-done.3.right), channel_id=1, source_target_pairs={{0,256},{256,512},{512,768},{768,0},{1,257},{257,513},{513,769},{7... | collective-permute-start | bytes 983048 | tf_op jit(solution)/shard_map/ppermute | solution.py:119
  83.5 23.7 %collective-permute-start.4 = (bf16[16,80,256]{2,1,0:T(8,128)(2,1)S(1)}, bf16[16,80,256]{2,1,0:T(8,128)(2,1)S(1)}, u32[]{:S(2)}, u32[]{:S(2)}) collective-permute-start(bf16[16,80,256]{2,1,0:T(8,128)(2,1)S(1)} %slice.9.own), channel_id=1, source_target_pairs={{0,256},{256,512},{512,768},{768,0},{1,257},{257,513},{513,769},{7... | collective-permute-start | bytes 1966088 | tf_op jit(solution)/shard_map/ppermute | solution.py:119
  86.2 21.0 %collective-permute-start.2 = (bf16[16,80,256]{2,1,0:T(8,128)(2,1)S(1)}, bf16[16,80,256]{2,1,0:T(8,128)(2,1)S(1)}, u32[]{:S(2)}, u32[]{:S(2)}) collective-permute-start(bf16[16,80,256]{2,1,0:T(8,128)(2,1)S(1)} %collective-permute-done.left), channel_id=1, source_target_pairs={{0,768},{256,0},{512,256},{768,512},{1,769},{257,1},{513,257},{769... | collective-permute-start | bytes 1966088 | tf_op jit(solution)/shard_map/ppermute | solution.py:122
  94.7 12.4 %copy-start = (f32[128]{0:T(128)S(1)}, f32[128]{0:T(128)}, u32[]{:S(2)}) copy-start(f32[128]{0:T(128)} %param.9) | copy-start | bytes 1540
  94.7 12.4 %copy-start.1 = (f32[128]{0:T(128)S(1)}, f32[128]{0:T(128)}, u32[]{:S(2)}) copy-start(f32[128]{0:T(128)} %param.10) | copy-start | bytes 1540
  94.7 12.4 %collective-permute-start.7 = (f32[256,256]{1,0:T(8,128)S(1)}, f32[256,256]{1,0:T(8,128)S(1)}, u32[]{:S(2)}, u32[]{:S(2)}) collective-permute-start(f32[256,256]{1,0:T(8,128)S(1)} %shard_map.79.own), channel_id=1, source_target_pairs={{0,1},{1,0},{2,3},{3,2},{4,5},{5,4},{6,7},{7,6},{8,9},{9,8},{10,11... | collective-permute-start | bytes 786440 | tf_op jit(solution)/shard_map/ppermute | solution.py:167

commit v4 on v3

--- a/solution.py
+++ b/solution.py
@@ -122,12 +122,13 @@
         return lax.ppermute(a, "x", [(x, (x - 1) % N_X) for x in range(N_X)])
 
     query_own, key_own = column[:, :q_rows], column[:, q_rows:]
+    query_own, where = lax.optimization_barrier((query_own, where))
     query_left = down(query_own)
-    key_own, where, cosine, sine = lax.optimization_barrier((key_own, where, cosine, sine))
     key_right, key_left = up(key_own), down(key_own)
-    key_right, query_own, bias = lax.optimization_barrier((key_right, query_own, bias))
+    key_right, query_own, cosine, sine, bias = lax.optimization_barrier((key_right, query_own, cosine, sine, bias))
     query_right = up(query_own)
     key_far = up(key_right)
+    mine, key_own = lax.optimization_barrier((mine, key_own))
     other = lax.ppermute(mine, "core", [(0, 1), (1, 0)])
     depth = N_X * N_Z * q_rows
     mine, other = (

time: 111 us -> 103 us (0.928)
  waiting for transfers between devices: 15.7 us -> 10.1 us
  local copies, waits for them, and re-layouts: 4.12 us -> 2.21 us
    ppermute x3, waiting for transfers between devices: 15.6 us -> 10.1 us  [up(): return lax.ppermute(a, 'x', [(x, (x + 1) % N_X) for x in range(N_X)])]
    ppermute x3, starting transfers between devices: 13.3 us -> 11.1 us  [down(): return lax.ppermute(a, 'x', [(x, (x - 1) % N_X) for x in range(N_X)])]
    ppermute x3, starting transfers between devices: 5.75 us -> 6.89 us  [up(): return lax.ppermute(a, 'x', [(x, (x + 1) % N_X) for x in range(N_X)])]
  transfers between devices with their start and end apart: 9 -> 9, of which waited for: 3 -> 2; matrix products, arithmetic and copies ran while one was open for 2% -> 1% of each run, Pallas kernels for 3% -> 4%
where the time goes in v4:
time: 103 us
  blocking collectives  42.5 us (41%)
  starting transfers between devices  39.1 us (38%)
  waiting for transfers between devices  10.1 us (10%)
  Pallas kernels  6.74 us (7%)
  local copies, waits for them, and re-layouts  2.21 us (2%)
  other arithmetic  1.06 us (1%)
    all_gather x1, blocking collectives, body(): column = lax.all_gather(block, 'z', axis=0)  42.5 us
    ppermute x3, starting transfers between devices, down(): return lax.ppermute(a, 'x', [(x, (x - 1) % N_X) for x in range(N_X)])  11.1 us
    ppermute x3, waiting for transfers between devices, up(): return lax.ppermute(a, 'x', [(x, (x + 1) % N_X) for x in range(N_X)])  10.1 us
    ppermute x1, starting transfers between devices, body(): other = lax.ppermute(mine, 'core', [(0, 1), (1, 0)])  9.51 us
    all_to_all x1, starting transfers between devices, body(): lax.all_to_all(jnp.broadcast_to(tokens[None], (N_YH * N_YL, *tokens.shape...  7.78 us
    ppermute x3, starting transfers between devices, up(): return lax.ppermute(a, 'x', [(x, (x + 1) % N_X) for x in range(N_X)])  6.89 us
    ppermute x1, starting transfers between devices, body(): partner = lax.ppermute(partial, 'yl', [(0, 1), (1, 0)])  3.84 us
    pallas_call x1, Pallas kernels, body(): pl.pallas_call(functools.partial(attend_kernel, head_size), out_shape=(ja...  2.9 us
  transfers between devices with their start and end apart: 9, of which 2 were waited for; matrix products, arithmetic and copies ran while one was open for 1% of the time, Pallas kernels for 4%

profile of v4, /device:TPU:1, one launch (start us, length us, event | category | flops | bytes accessed | tf_op | source)
XLA Modules:
  0.0 102.6 jit_solution(9156541201212064221)
XLA Ops:
  0.6 2.1 %broadcast_in_dim.27 = bf16[8,16,5120]{2,1,0:T(8,128)(2,1)} broadcast(bf16[16,5120]{1,0:T(8,128)(2,1)} %param.6), dimensions={1,2} | broadcast | bytes 1474560 | tf_op jit(solution)/shard_map/broadcast_in_dim | solution.py:100
  2.7 0.0 copy-start.2
  2.7 0.0 copy-start.3
  2.7 7.8 %all-to-all-start = ((bf16[8,16,5120]{2,1,0:T(8,128)(2,1)}), bf16[8,16,5120]{2,1,0:T(8,128)(2,1)S(1)}, u32[]{:S(2)}, u32[]{:S(2)}) async-start(bf16[8,16,5120]{2,1,0:T(8,128)(2,1)} %broadcast_in_dim.27), calls=%async_computation | async-start | bytes 2621440 | tf_op jit(solution)/shard_map/all_to_all | solution.py:99
  10.5 0.0 copy-done.2
  10.5 0.0 copy-done.3
  10.6 0.0 copy-start.4
  10.6 42.5 %all-gather = bf16[1920,256]{1,0:T(8,128)(2,1)S(1)} all-gather(bf16[120,256]{1,0:T(8,128)(2,1)S(1)} %pad_maximum_fusion.2), channel_id=2, replica_groups=mesh['x'=4,'z'=16,'yh'=4,'core'=2,'yl'=2] {'z'}, dimensions={0}, use_global_device_ids=true | all-gather | bytes 1044480 | tf_op jit(solution)/shard_map/all_gather | solution.py:117
  53.1 2.9 %collective-permute-start.3 = (bf16[16,40,256]{2,1,0:T(8,128)(2,1)S(1)}, bf16[16,40,256]{2,1,0:T(8,128)(2,1)S(1)}, u32[]{:S(2)}, u32[]{:S(2)}) collective-permute-start(bf16[16,40,256]{2,1,0:T(8,128)(2,1)S(1)} %slice.9.own), channel_id=1, source_target_pairs={{0,256},{256,512},{512,768},{768,0},{1,257},{257,513},{513,769},{7... | collective-permute-start | bytes 983048 | tf_op jit(solution)/shard_map/ppermute | solution.py:119
  55.9 3.6 %collective-permute-start.5 = (bf16[16,40,256]{2,1,0:T(8,128)(2,1)S(1)}, bf16[16,40,256]{2,1,0:T(8,128)(2,1)}, u32[]{:S(2)}, u32[]{:S(2)}) collective-permute-start(bf16[16,40,256]{2,1,0:T(8,128)(2,1)S(1)} %slice.9.own), channel_id=1, source_target_pairs={{0,768},{256,0},{512,256},{768,512},{1,769},{257,1},{513,257},{769... | collective-permute-start | bytes 983048 | tf_op jit(solution)/shard_map/ppermute | solution.py:122
  59.6 0.1 pad_add_fusion.where
  59.7 2.9 %collective-permute-start = (bf16[16,80,256]{2,1,0:T(8,128)(2,1)S(1)}, bf16[16,80,256]{2,1,0:T(8,128)(2,1)S(1)}, u32[]{:S(2)}, u32[]{:S(2)}) collective-permute-start(bf16[16,80,256]{2,1,0:T(8,128)(2,1)S(1)} %slice.8.own), channel_id=1, source_target_pairs={{0,768},{256,0},{512,256},{768,512},{1,769},{257,1},{513,257},{769... | collective-permute-start | bytes 1966088 | tf_op jit(solution)/shard_map/ppermute | solution.py:122
  62.6 0.0 all-to-all-done
  62.6 9.5 %collective-permute-start.1 = (bf16[8,16,5120]{2,1,0:T(8,128)(2,1)S(1)}, bf16[8,16,5120]{2,1,0:T(8,128)(2,1)S(1)}, u32[]{:S(2)}, u32[]{:S(2)}) collective-permute-start(bf16[8,16,5120]{2,1,0:T(8,128)(2,1)S(1)} %all-to-all-done), channel_id=1, source_target_pairs={{0,2},{2,0},{1,3},{3,1},{4,6},{6,4},{5,7},{7,5},{8,10},{10,8},{9,1... | collective-permute-start | bytes 3932168 | tf_op jit(solution)/shard_map/ppermute | solution.py:132
  72.2 0.0 copy-done.4
  72.2 0.2 convert_reduce_fusion
  72.4 0.5 fusion.2
  72.9 0.1 pad_maximum_fusion
  73.1 0.1 fusion.1.bias
  73.2 0.0 collective-permute-done.3.right
  73.2 2.1 %collective-permute-start.6 = (bf16[16,40,256]{2,1,0:T(8,128)(2,1)S(1)}, bf16[16,40,256]{2,1,0:T(8,128)(2,1)S(1)}, u32[]{:S(2)}, u32[]{:S(2)}) collective-permute-start(bf16[16,40,256]{2,1,0:T(8,128)(2,1)S(1)} %collective-permute-done.3.right), channel_id=1, source_target_pairs={{0,256},{256,512},{512,768},{768,0},{1,257},{257,513},{513,769},{7... | collective-permute-start | bytes 983048 | tf_op jit(solution)/shard_map/ppermute | solution.py:119
  75.3 1.9 %collective-permute-start.4 = (bf16[16,80,256]{2,1,0:T(8,128)(2,1)S(1)}, bf16[16,80,256]{2,1,0:T(8,128)(2,1)S(1)}, u32[]{:S(2)}, u32[]{:S(2)}) collective-permute-start(bf16[16,80,256]{2,1,0:T(8,128)(2,1)S(1)} %slice.8.own), channel_id=1, source_target_pairs={{0,256},{256,512},{512,768},{768,0},{1,257},{257,513},{513,769},{7... | collective-permute-start | bytes 1966088 | tf_op jit(solution)/shard_map/ppermute | solution.py:119
  77.2 0.0 collective-permute-done.1
  77.2 0.7 shard_map.77.held
  78.0 0.0 collective-permute-done.left
  78.0 4.6 %collective-permute-start.2 = (bf16[16,80,256]{2,1,0:T(8,128)(2,1)S(1)}, bf16[16,80,256]{2,1,0:T(8,128)(2,1)S(1)}, u32[]{:S(2)}, u32[]{:S(2)}) collective-permute-start(bf16[16,80,256]{2,1,0:T(8,128)(2,1)S(1)} %collective-permute-done.left), channel_id=1, source_target_pairs={{0,768},{256,0},{512,256},{768,512},{1,769},{257,1},{513,257},{769... | collective-permute-start | bytes 1966088 | tf_op jit(solution)/shard_map/ppermute | solution.py:122
  82.6 0.0 collective-permute-done.5.left
  82.6 3.0 %collective-permute-done.6.far = bf16[16,40,256]{2,1,0:T(8,128)(2,1)S(1)} collective-permute-done((bf16[16,40,256]{2,1,0:T(8,128)(2,1)S(1)}, bf16[16,40,256]{2,1,0:T(8,128)(2,1)S(1)}, u32[]{:S(2)}, u32[]{:S(2)}) %collective-permute-start.6) | collective-permute-done | bytes 327712 | tf_op jit(solution)/shard_map/ppermute | solution.py:119
  85.6 2.0 %shard_map.79.own = f32[256,256]{1,0:T(8,128)S(1)} custom-call(s32[3]{0:T(128)S(1)} %pad_add_fusion.where, bf16[4,2,2,16,5120]{4,3,2,1,0:T(8,128)(2,1)S(1)} %shard_map.77.held, bf16[16,40,256]{2,1,0:T(8,128)(2,1)S(1)} %slice.9.own, bf16[16,40,256]{2,1,0:T(8,128)(2,1)S(1)} %collective-permute-done.3.right, bf16[16,40,256]{2,1,0:T(8,128)(2,1)} %collective-permute-done.5.left, ...), custom_call_target="tpu_custom_call" | custom-call | flops 6710886400 | bytes 52428800 | tf_op jit(solution)/shard_map/pallas_call | solution.py:160
  87.7 0.0 copy-start
  87.7 0.0 copy-start.1
  87.7 3.8 %collective-permute-start.7 = (f32[256,256]{1,0:T(8,128)S(1)}, f32[256,256]{1,0:T(8,128)S(1)}, u32[]{:S(2)}, u32[]{:S(2)}) collective-permute-start(f32[256,256]{1,0:T(8,128)S(1)} %shard_map.79.own), channel_id=1, source_target_pairs={{0,1},{1,0},{2,3},{3,2},{4,5},{5,4},{6,7},{7,6},{8,9},{9,8},{10,11... | collective-permute-start | bytes 786440 | tf_op jit(solution)/shard_map/ppermute | solution.py:168
  91.5 1.1 %shard_map.78.near = f32[256,256]{1,0:T(8,128)S(1)} custom-call(s32[3]{0:T(128)S(1)} %pad_add_fusion.where, bf16[4,2,2,16,5120]{4,3,2,1,0:T(8,128)(2,1)S(1)} %shard_map.77.held, bf16[16,80,256]{2,1,0:T(8,128)(2,1)S(1)} %slice.8.own, bf16[16,80,256]{2,1,0:T(8,128)(2,1)S(1)} %collective-permute-done.left), custom_call_target="tpu_custom_call" | custom-call | flops 3355443200 | bytes 26214400 | tf_op jit(solution)/shard_map/pallas_call | solution.py:169
  92.6 7.1 %collective-permute-done.4.right = bf16[16,80,256]{2,1,0:T(8,128)(2,1)S(1)} collective-permute-done((bf16[16,80,256]{2,1,0:T(8,128)(2,1)S(1)}, bf16[16,80,256]{2,1,0:T(8,128)(2,1)S(1)}, u32[]{:S(2)}, u32[]{:S(2)}) %collective-permute-start.4) | collective-permute-done | bytes 655392 | tf_op jit(solution)/shard_map/ppermute | solution.py:119
  99.7 0.0 collective-permute-done.7.partner
  99.7 0.0 collective-permute-done.2.far
  99.7 0.0 copy-done
  99.7 0.0 copy-done.1
  99.7 2.9 %shard_map.80 = (bf16[256,256]{1,0:T(8,128)(2,1)}, bf16[256,256]{1,0:T(8,128)(2,1)}) custom-call(s32[3]{0:T(128)S(1)} %pad_add_fusion.where, bf16[4,2,2,16,5120]{4,3,2,1,0:T(8,128)(2,1)S(1)} %shard_map.77.held, bf16[16,80,256]{2,1,0:T(8,128)(2,1)S(1)} %collective-permute-done.2.far, bf16[16,80,256]{2,1,0:T(8,128)(2,1)S(1)} %collective-permute-done.4.right, ...), custom_call_target="tpu_custom_call" | custom-call | flops 3355443200 | bytes 26214400 | tf_op jit(solution)/shard_map/pallas_call | solution.py:176
  (5 shorter events, 0.1 us)
Async XLA Ops:
  2.7 7.8 %copy-start.2 = (bf16[80,256]{1,0:T(8,128)(2,1)S(1)}, bf16[80,256]{1,0:T(8,128)(2,1)}, u32[]{:S(2)}) copy-start(bf16[80,256]{1,0:T(8,128)(2,1)} %param.7) | copy-start | bytes 122884
  2.7 7.8 %copy-start.3 = (bf16[40,1,256]{2,0,1:T(8,128)(2,1)S(1)}, bf16[40,1,256]{2,0,1:T(8,128)(2,1)}, u32[]{:S(2)}) copy-start(bf16[40,1,256]{2,0,1:T(8,128)(2,1)} %param.8) | copy-start | bytes 61444
  2.7 59.9 %all-to-all-start = ((bf16[8,16,5120]{2,1,0:T(8,128)(2,1)}), bf16[8,16,5120]{2,1,0:T(8,128)(2,1)S(1)}, u32[]{:S(2)}, u32[]{:S(2)}) async-start(bf16[8,16,5120]{2,1,0:T(8,128)(2,1)} %broadcast_in_dim.27), calls=%async_computation | async-start | bytes 2621440 | tf_op jit(solution)/shard_map/all_to_all | solution.py:99
  10.6 61.6 %copy-start.4 = (s32[1,256]{1,0:T(1,128)S(1)}, s32[1,256]{1,0:T(1,128)}, u32[]{:S(2)}) copy-start(s32[1,256]{1,0:T(1,128)} %param.11) | copy-start | bytes 3076
  53.1 20.1 %collective-permute-start.3 = (bf16[16,40,256]{2,1,0:T(8,128)(2,1)S(1)}, bf16[16,40,256]{2,1,0:T(8,128)(2,1)S(1)}, u32[]{:S(2)}, u32[]{:S(2)}) collective-permute-start(bf16[16,40,256]{2,1,0:T(8,128)(2,1)S(1)} %slice.9.own), channel_id=1, source_target_pairs={{0,256},{256,512},{512,768},{768,0},{1,257},{257,513},{513,769},{7... | collective-permute-start | bytes 983048 | tf_op jit(solution)/shard_map/ppermute | solution.py:119
  55.9 26.6 %collective-permute-start.5 = (bf16[16,40,256]{2,1,0:T(8,128)(2,1)S(1)}, bf16[16,40,256]{2,1,0:T(8,128)(2,1)}, u32[]{:S(2)}, u32[]{:S(2)}) collective-permute-start(bf16[16,40,256]{2,1,0:T(8,128)(2,1)S(1)} %slice.9.own), channel_id=1, source_target_pairs={{0,768},{256,0},{512,256},{768,512},{1,769},{257,1},{513,257},{769... | collective-permute-start | bytes 983048 | tf_op jit(solution)/shard_map/ppermute | solution.py:122
  59.7 18.3 %collective-permute-start = (bf16[16,80,256]{2,1,0:T(8,128)(2,1)S(1)}, bf16[16,80,256]{2,1,0:T(8,128)(2,1)S(1)}, u32[]{:S(2)}, u32[]{:S(2)}) collective-permute-start(bf16[16,80,256]{2,1,0:T(8,128)(2,1)S(1)} %slice.8.own), channel_id=1, source_target_pairs={{0,768},{256,0},{512,256},{768,512},{1,769},{257,1},{513,257},{769... | collective-permute-start | bytes 1966088 | tf_op jit(solution)/shard_map/ppermute | solution.py:122
  62.6 14.6 %collective-permute-start.1 = (bf16[8,16,5120]{2,1,0:T(8,128)(2,1)S(1)}, bf16[8,16,5120]{2,1,0:T(8,128)(2,1)S(1)}, u32[]{:S(2)}, u32[]{:S(2)}) collective-permute-start(bf16[8,16,5120]{2,1,0:T(8,128)(2,1)S(1)} %all-to-all-done), channel_id=1, source_target_pairs={{0,2},{2,0},{1,3},{3,1},{4,6},{6,4},{5,7},{7,5},{8,10},{10,8},{9,1... | collective-permute-start | bytes 3932168 | tf_op jit(solution)/shard_map/ppermute | solution.py:132
  73.2 12.4 %collective-permute-start.6 = (bf16[16,40,256]{2,1,0:T(8,128)(2,1)S(1)}, bf16[16,40,256]{2,1,0:T(8,128)(2,1)S(1)}, u32[]{:S(2)}, u32[]{:S(2)}) collective-permute-start(bf16[16,40,256]{2,1,0:T(8,128)(2,1)S(1)} %collective-permute-done.3.right), channel_id=1, source_target_pairs={{0,256},{256,512},{512,768},{768,0},{1,257},{257,513},{513,769},{7... | collective-permute-start | bytes 983048 | tf_op jit(solution)/shard_map/ppermute | solution.py:119
  75.3 24.4 %collective-permute-start.4 = (bf16[16,80,256]{2,1,0:T(8,128)(2,1)S(1)}, bf16[16,80,256]{2,1,0:T(8,128)(2,1)S(1)}, u32[]{:S(2)}, u32[]{:S(2)}) collective-permute-start(bf16[16,80,256]{2,1,0:T(8,128)(2,1)S(1)} %slice.8.own), channel_id=1, source_target_pairs={{0,256},{256,512},{512,768},{768,0},{1,257},{257,513},{513,769},{7... | collective-permute-start | bytes 1966088 | tf_op jit(solution)/shard_map/ppermute | solution.py:119
  78.0 21.7 %collective-permute-start.2 = (bf16[16,80,256]{2,1,0:T(8,128)(2,1)S(1)}, bf16[16,80,256]{2,1,0:T(8,128)(2,1)S(1)}, u32[]{:S(2)}, u32[]{:S(2)}) collective-permute-start(bf16[16,80,256]{2,1,0:T(8,128)(2,1)S(1)} %collective-permute-done.left), channel_id=1, source_target_pairs={{0,768},{256,0},{512,256},{768,512},{1,769},{257,1},{513,257},{769... | collective-permute-start | bytes 1966088 | tf_op jit(solution)/shard_map/ppermute | solution.py:122
  87.7 12.0 %copy-start = (f32[128]{0:T(128)S(1)}, f32[128]{0:T(128)}, u32[]{:S(2)}) copy-start(f32[128]{0:T(128)} %param.9) | copy-start | bytes 1540
  87.7 12.0 %copy-start.1 = (f32[128]{0:T(128)S(1)}, f32[128]{0:T(128)}, u32[]{:S(2)}) copy-start(f32[128]{0:T(128)} %param.10) | copy-start | bytes 1540
  87.7 12.0 %collective-permute-start.7 = (f32[256,256]{1,0:T(8,128)S(1)}, f32[256,256]{1,0:T(8,128)S(1)}, u32[]{:S(2)}, u32[]{:S(2)}) collective-permute-start(f32[256,256]{1,0:T(8,128)S(1)} %shard_map.79.own), channel_id=1, source_target_pairs={{0,1},{1,0},{2,3},{3,2},{4,5},{5,4},{6,7},{7,6},{8,9},{9,8},{10,11... | collective-permute-start | bytes 786440 | tf_op jit(solution)/shard_map/ppermute | solution.py:168

commit v5 on v4

--- a/solution.py
+++ b/solution.py
@@ -123,10 +123,11 @@
 
     query_own, key_own = column[:, :q_rows], column[:, q_rows:]
     query_own, where = lax.optimization_barrier((query_own, where))
-    query_left = down(query_own)
-    key_right, key_left = up(key_own), down(key_own)
-    key_right, query_own, cosine, sine, bias = lax.optimization_barrier((key_right, query_own, cosine, sine, bias))
-    query_right = up(query_own)
+    key_right, query_left = up(key_own), down(query_own)
+    key_last, cosine, sine = lax.optimization_barrier((key_own, cosine, sine))
+    key_left = down(key_last)
+    key_right, query_last, bias = lax.optimization_barrier((key_right, query_own, bias))
+    query_right = up(query_last)
     key_far = up(key_right)
     mine, key_own = lax.optimization_barrier((mine, key_own))
     other = lax.ppermute(mine, "core", [(0, 1), (1, 0)])

time: 103 us -> 104 us (level)
    ppermute x3, starting transfers between devices: 11.1 us -> 13.5 us  [down(): return lax.ppermute(a, 'x', [(x, (x - 1) % N_X) for x in range(N_X)])]
    ppermute x3, starting transfers between devices: 6.89 us -> 5.76 us  [up(): return lax.ppermute(a, 'x', [(x, (x + 1) % N_X) for x in range(N_X)])]
  transfers between devices with their start and end apart: 9 -> 9, of which waited for: 2 -> 2; matrix products, arithmetic and copies ran while one was open for 1% -> 1% of each run, Pallas kernels for 4% -> 3%
where the time goes in v5:
time: 104 us; the launch traced here: 103 us
  blocking collectives  42.5 us (41%)
  starting transfers between devices  39.9 us (38%)
  waiting for transfers between devices  10.2 us (10%)
  Pallas kernels  6.3 us (6%)
  local copies, waits for them, and re-layouts  2.21 us (2%)
  other arithmetic  1.06 us (1%)
    all_gather x1, blocking collectives, body(): column = lax.all_gather(block, 'z', axis=0)  42.5 us
    ppermute x3, starting transfers between devices, down(): return lax.ppermute(a, 'x', [(x, (x - 1) % N_X) for x in range(N_X)])  13.5 us
    ppermute x3, waiting for transfers between devices, up(): return lax.ppermute(a, 'x', [(x, (x + 1) % N_X) for x in range(N_X)])  10.2 us
    ppermute x1, starting transfers between devices, body(): other = lax.ppermute(mine, 'core', [(0, 1), (1, 0)])  8.95 us
    all_to_all x1, starting transfers between devices, body(): lax.all_to_all(jnp.broadcast_to(tokens[None], (N_YH * N_YL, *tokens.shape...  7.78 us
    ppermute x3, starting transfers between devices, up(): return lax.ppermute(a, 'x', [(x, (x + 1) % N_X) for x in range(N_X)])  5.76 us
    ppermute x1, starting transfers between devices, body(): partner = lax.ppermute(partial, 'yl', [(0, 1), (1, 0)])  3.84 us
    pallas_call x1, Pallas kernels, body(): pl.pallas_call(functools.partial(attend_kernel, head_size), out_shape=(ja...  2.89 us
  transfers between devices with their start and end apart: 9, of which 2 were waited for; matrix products, arithmetic and copies ran while one was open for 1% of the time, Pallas kernels for 3%

profile of v5, /device:TPU:1, one launch (start us, length us, event | category | flops | bytes accessed | tf_op | source)
XLA Modules:
  0.0 103.0 jit_solution(10806664150693941331)
XLA Ops:
  0.6 2.1 %broadcast_in_dim.27 = bf16[8,16,5120]{2,1,0:T(8,128)(2,1)} broadcast(bf16[16,5120]{1,0:T(8,128)(2,1)} %param.6), dimensions={1,2} | broadcast | bytes 1474560 | tf_op jit(solution)/shard_map/broadcast_in_dim | solution.py:100
  2.7 0.0 copy-start.2
  2.7 0.0 copy-start.3
  2.7 7.8 %all-to-all-start = ((bf16[8,16,5120]{2,1,0:T(8,128)(2,1)}), bf16[8,16,5120]{2,1,0:T(8,128)(2,1)S(1)}, u32[]{:S(2)}, u32[]{:S(2)}) async-start(bf16[8,16,5120]{2,1,0:T(8,128)(2,1)} %broadcast_in_dim.27), calls=%async_computation | async-start | bytes 2621440 | tf_op jit(solution)/shard_map/all_to_all | solution.py:99
  10.5 0.0 copy-done.2
  10.5 0.0 copy-done.3
  10.6 0.0 copy-start.4
  10.6 42.5 %all-gather = bf16[1920,256]{1,0:T(8,128)(2,1)S(1)} all-gather(bf16[120,256]{1,0:T(8,128)(2,1)S(1)} %pad_maximum_fusion.2), channel_id=2, replica_groups=mesh['x'=4,'z'=16,'yh'=4,'core'=2,'yl'=2] {'z'}, dimensions={0}, use_global_device_ids=true | all-gather | bytes 1044480 | tf_op jit(solution)/shard_map/all_gather | solution.py:117
  53.1 0.1 pad_add_fusion.where
  53.2 4.1 %collective-permute-start = (bf16[16,80,256]{2,1,0:T(8,128)(2,1)S(1)}, bf16[16,80,256]{2,1,0:T(8,128)(2,1)S(1)}, u32[]{:S(2)}, u32[]{:S(2)}) collective-permute-start(bf16[16,80,256]{2,1,0:T(8,128)(2,1)S(1)} %slice.8.own), channel_id=1, source_target_pairs={{0,768},{256,0},{512,256},{768,512},{1,769},{257,1},{513,257},{769... | collective-permute-start | bytes 1966088 | tf_op jit(solution)/shard_map/ppermute | solution.py:122
  57.3 1.9 %collective-permute-start.3 = (bf16[16,40,256]{2,1,0:T(8,128)(2,1)S(1)}, bf16[16,40,256]{2,1,0:T(8,128)(2,1)S(1)}, u32[]{:S(2)}, u32[]{:S(2)}) collective-permute-start(bf16[16,40,256]{2,1,0:T(8,128)(2,1)S(1)} %slice.9.own), channel_id=1, source_target_pairs={{0,256},{256,512},{512,768},{768,0},{1,257},{257,513},{513,769},{7... | collective-permute-start | bytes 983048 | tf_op jit(solution)/shard_map/ppermute | solution.py:119
  59.3 0.0 all-to-all-done
  59.3 8.9 %collective-permute-start.1 = (bf16[8,16,5120]{2,1,0:T(8,128)(2,1)S(1)}, bf16[8,16,5120]{2,1,0:T(8,128)(2,1)S(1)}, u32[]{:S(2)}, u32[]{:S(2)}) collective-permute-start(bf16[8,16,5120]{2,1,0:T(8,128)(2,1)S(1)} %all-to-all-done), channel_id=1, source_target_pairs={{0,2},{2,0},{1,3},{3,1},{4,6},{6,4},{5,7},{7,5},{8,10},{10,8},{9,1... | collective-permute-start | bytes 3932168 | tf_op jit(solution)/shard_map/ppermute | solution.py:133
  68.2 0.0 copy-done.4
  68.2 0.2 convert_reduce_fusion
  68.4 0.5 fusion.2
  69.0 0.1 pad_maximum_fusion
  69.1 4.9 %collective-permute-start.5 = (bf16[16,40,256]{2,1,0:T(8,128)(2,1)S(1)}, bf16[16,40,256]{2,1,0:T(8,128)(2,1)S(1)}, u32[]{:S(2)}, u32[]{:S(2)}) collective-permute-start(bf16[16,40,256]{2,1,0:T(8,128)(2,1)S(1)} %slice.9.own), channel_id=1, source_target_pairs={{0,768},{256,0},{512,256},{768,512},{1,769},{257,1},{513,257},{769... | collective-permute-start | bytes 983048 | tf_op jit(solution)/shard_map/ppermute | solution.py:122
  74.0 0.1 fusion.1.bias
  74.1 0.0 collective-permute-done.3.right
  74.1 1.9 %collective-permute-start.6 = (bf16[16,40,256]{2,1,0:T(8,128)(2,1)S(1)}, bf16[16,40,256]{2,1,0:T(8,128)(2,1)S(1)}, u32[]{:S(2)}, u32[]{:S(2)}) collective-permute-start(bf16[16,40,256]{2,1,0:T(8,128)(2,1)S(1)} %collective-permute-done.3.right), channel_id=1, source_target_pairs={{0,256},{256,512},{512,768},{768,0},{1,257},{257,513},{513,769},{7... | collective-permute-start | bytes 983048 | tf_op jit(solution)/shard_map/ppermute | solution.py:119
  76.0 1.9 %collective-permute-start.4 = (bf16[16,80,256]{2,1,0:T(8,128)(2,1)S(1)}, bf16[16,80,256]{2,1,0:T(8,128)(2,1)S(1)}, u32[]{:S(2)}, u32[]{:S(2)}) collective-permute-start(bf16[16,80,256]{2,1,0:T(8,128)(2,1)S(1)} %slice.8.own), channel_id=1, source_target_pairs={{0,256},{256,512},{512,768},{768,0},{1,257},{257,513},{513,769},{7... | collective-permute-start | bytes 1966088 | tf_op jit(solution)/shard_map/ppermute | solution.py:119
  78.0 0.0 collective-permute-done.1
  78.0 0.7 shard_map.77.held
  78.7 0.0 collective-permute-done.left
  78.7 4.6 %collective-permute-start.2 = (bf16[16,80,256]{2,1,0:T(8,128)(2,1)S(1)}, bf16[16,80,256]{2,1,0:T(8,128)(2,1)S(1)}, u32[]{:S(2)}, u32[]{:S(2)}) collective-permute-start(bf16[16,80,256]{2,1,0:T(8,128)(2,1)S(1)} %collective-permute-done.left), channel_id=1, source_target_pairs={{0,768},{256,0},{512,256},{768,512},{1,769},{257,1},{513,257},{769... | collective-permute-start | bytes 1966088 | tf_op jit(solution)/shard_map/ppermute | solution.py:122
  83.3 0.0 collective-permute-done.5.left
  83.3 2.7 %collective-permute-done.6.far = bf16[16,40,256]{2,1,0:T(8,128)(2,1)S(1)} collective-permute-done((bf16[16,40,256]{2,1,0:T(8,128)(2,1)S(1)}, bf16[16,40,256]{2,1,0:T(8,128)(2,1)S(1)}, u32[]{:S(2)}, u32[]{:S(2)}) %collective-permute-start.6) | collective-permute-done | bytes 327712 | tf_op jit(solution)/shard_map/ppermute | solution.py:119
  86.1 1.6 %shard_map.79.own = f32[256,256]{1,0:T(8,128)S(1)} custom-call(s32[3]{0:T(128)S(1)} %pad_add_fusion.where, bf16[4,2,2,16,5120]{4,3,2,1,0:T(8,128)(2,1)S(1)} %shard_map.77.held, bf16[16,40,256]{2,1,0:T(8,128)(2,1)S(1)} %slice.9.own, bf16[16,40,256]{2,1,0:T(8,128)(2,1)S(1)} %collective-permute-done.3.right, ...), custom_call_target="tpu_custom_call" | custom-call | flops 6710886400 | bytes 52428800 | tf_op jit(solution)/shard_map/pallas_call | solution.py:161
  87.7 0.0 copy-start
  87.7 0.0 copy-start.1
  87.7 3.8 %collective-permute-start.7 = (f32[256,256]{1,0:T(8,128)S(1)}, f32[256,256]{1,0:T(8,128)S(1)}, u32[]{:S(2)}, u32[]{:S(2)}) collective-permute-start(f32[256,256]{1,0:T(8,128)S(1)} %shard_map.79.own), channel_id=1, source_target_pairs={{0,1},{1,0},{2,3},{3,2},{4,5},{5,4},{6,7},{7,6},{8,9},{9,8},{10,11... | collective-permute-start | bytes 786440 | tf_op jit(solution)/shard_map/ppermute | solution.py:169
  91.5 1.1 %shard_map.78.near = f32[256,256]{1,0:T(8,128)S(1)} custom-call(s32[3]{0:T(128)S(1)} %pad_add_fusion.where, bf16[4,2,2,16,5120]{4,3,2,1,0:T(8,128)(2,1)S(1)} %shard_map.77.held, bf16[16,80,256]{2,1,0:T(8,128)(2,1)S(1)} %slice.8.own, bf16[16,80,256]{2,1,0:T(8,128)(2,1)S(1)} %collective-permute-done.left), custom_call_target="tpu_custom_call" | custom-call | flops 3355443200 | bytes 26214400 | tf_op jit(solution)/shard_map/pallas_call | solution.py:170
  92.6 7.5 %collective-permute-done.4.right = bf16[16,80,256]{2,1,0:T(8,128)(2,1)S(1)} collective-permute-done((bf16[16,80,256]{2,1,0:T(8,128)(2,1)S(1)}, bf16[16,80,256]{2,1,0:T(8,128)(2,1)S(1)}, u32[]{:S(2)}, u32[]{:S(2)}) %collective-permute-start.4) | collective-permute-done | bytes 655392 | tf_op jit(solution)/shard_map/ppermute | solution.py:119
  100.1 0.0 collective-permute-done.7.partner
  100.1 0.0 collective-permute-done.2.far
  100.1 0.0 copy-done
  100.1 0.0 copy-done.1
  100.1 2.9 %shard_map.80 = (bf16[256,256]{1,0:T(8,128)(2,1)}, bf16[256,256]{1,0:T(8,128)(2,1)}) custom-call(s32[3]{0:T(128)S(1)} %pad_add_fusion.where, bf16[4,2,2,16,5120]{4,3,2,1,0:T(8,128)(2,1)S(1)} %shard_map.77.held, bf16[16,80,256]{2,1,0:T(8,128)(2,1)S(1)} %collective-permute-done.2.far, bf16[16,80,256]{2,1,0:T(8,128)(2,1)S(1)} %collective-permute-done.4.right, ...), custom_call_target="tpu_custom_call" | custom-call | flops 3355443200 | bytes 26214400 | tf_op jit(solution)/shard_map/pallas_call | solution.py:177
  (5 shorter events, 0.1 us)
Async XLA Ops:
  2.7 7.8 %copy-start.2 = (bf16[80,256]{1,0:T(8,128)(2,1)S(1)}, bf16[80,256]{1,0:T(8,128)(2,1)}, u32[]{:S(2)}) copy-start(bf16[80,256]{1,0:T(8,128)(2,1)} %param.7) | copy-start | bytes 122884
  2.7 7.8 %copy-start.3 = (bf16[40,1,256]{2,0,1:T(8,128)(2,1)S(1)}, bf16[40,1,256]{2,0,1:T(8,128)(2,1)}, u32[]{:S(2)}) copy-start(bf16[40,1,256]{2,0,1:T(8,128)(2,1)} %param.8) | copy-start | bytes 61444
  2.7 56.5 %all-to-all-start = ((bf16[8,16,5120]{2,1,0:T(8,128)(2,1)}), bf16[8,16,5120]{2,1,0:T(8,128)(2,1)S(1)}, u32[]{:S(2)}, u32[]{:S(2)}) async-start(bf16[8,16,5120]{2,1,0:T(8,128)(2,1)} %broadcast_in_dim.27), calls=%async_computation | async-start | bytes 2621440 | tf_op jit(solution)/shard_map/all_to_all | solution.py:99
  10.6 57.7 %copy-start.4 = (s32[1,256]{1,0:T(1,128)S(1)}, s32[1,256]{1,0:T(1,128)}, u32[]{:S(2)}) copy-start(s32[1,256]{1,0:T(1,128)} %param.11) | copy-start | bytes 3076
  53.2 25.6 %collective-permute-start = (bf16[16,80,256]{2,1,0:T(8,128)(2,1)S(1)}, bf16[16,80,256]{2,1,0:T(8,128)(2,1)S(1)}, u32[]{:S(2)}, u32[]{:S(2)}) collective-permute-start(bf16[16,80,256]{2,1,0:T(8,128)(2,1)S(1)} %slice.8.own), channel_id=1, source_target_pairs={{0,768},{256,0},{512,256},{768,512},{1,769},{257,1},{513,257},{769... | collective-permute-start | bytes 1966088 | tf_op jit(solution)/shard_map/ppermute | solution.py:122
  57.3 16.8 %collective-permute-start.3 = (bf16[16,40,256]{2,1,0:T(8,128)(2,1)S(1)}, bf16[16,40,256]{2,1,0:T(8,128)(2,1)S(1)}, u32[]{:S(2)}, u32[]{:S(2)}) collective-permute-start(bf16[16,40,256]{2,1,0:T(8,128)(2,1)S(1)} %slice.9.own), channel_id=1, source_target_pairs={{0,256},{256,512},{512,768},{768,0},{1,257},{257,513},{513,769},{7... | collective-permute-start | bytes 983048 | tf_op jit(solution)/shard_map/ppermute | solution.py:119
  59.3 18.7 %collective-permute-start.1 = (bf16[8,16,5120]{2,1,0:T(8,128)(2,1)S(1)}, bf16[8,16,5120]{2,1,0:T(8,128)(2,1)S(1)}, u32[]{:S(2)}, u32[]{:S(2)}) collective-permute-start(bf16[8,16,5120]{2,1,0:T(8,128)(2,1)S(1)} %all-to-all-done), channel_id=1, source_target_pairs={{0,2},{2,0},{1,3},{3,1},{4,6},{6,4},{5,7},{7,5},{8,10},{10,8},{9,1... | collective-permute-start | bytes 3932168 | tf_op jit(solution)/shard_map/ppermute | solution.py:133
  69.1 14.2 %collective-permute-start.5 = (bf16[16,40,256]{2,1,0:T(8,128)(2,1)S(1)}, bf16[16,40,256]{2,1,0:T(8,128)(2,1)S(1)}, u32[]{:S(2)}, u32[]{:S(2)}) collective-permute-start(bf16[16,40,256]{2,1,0:T(8,128)(2,1)S(1)} %slice.9.own), channel_id=1, source_target_pairs={{0,768},{256,0},{512,256},{768,512},{1,769},{257,1},{513,257},{769... | collective-permute-start | bytes 983048 | tf_op jit(solution)/shard_map/ppermute | solution.py:122
  74.1 12.0 %collective-permute-start.6 = (bf16[16,40,256]{2,1,0:T(8,128)(2,1)S(1)}, bf16[16,40,256]{2,1,0:T(8,128)(2,1)S(1)}, u32[]{:S(2)}, u32[]{:S(2)}) collective-permute-start(bf16[16,40,256]{2,1,0:T(8,128)(2,1)S(1)} %collective-permute-done.3.right), channel_id=1, source_target_pairs={{0,256},{256,512},{512,768},{768,0},{1,257},{257,513},{513,769},{7... | collective-permute-start | bytes 983048 | tf_op jit(solution)/shard_map/ppermute | solution.py:119
  76.0 24.1 %collective-permute-start.4 = (bf16[16,80,256]{2,1,0:T(8,128)(2,1)S(1)}, bf16[16,80,256]{2,1,0:T(8,128)(2,1)S(1)}, u32[]{:S(2)}, u32[]{:S(2)}) collective-permute-start(bf16[16,80,256]{2,1,0:T(8,128)(2,1)S(1)} %slice.8.own), channel_id=1, source_target_pairs={{0,256},{256,512},{512,768},{768,0},{1,257},{257,513},{513,769},{7... | collective-permute-start | bytes 1966088 | tf_op jit(solution)/shard_map/ppermute | solution.py:119
  78.7 21.4 %collective-permute-start.2 = (bf16[16,80,256]{2,1,0:T(8,128)(2,1)S(1)}, bf16[16,80,256]{2,1,0:T(8,128)(2,1)S(1)}, u32[]{:S(2)}, u32[]{:S(2)}) collective-permute-start(bf16[16,80,256]{2,1,0:T(8,128)(2,1)S(1)} %collective-permute-done.left), channel_id=1, source_target_pairs={{0,768},{256,0},{512,256},{768,512},{1,769},{257,1},{513,257},{769... | collective-permute-start | bytes 1966088 | tf_op jit(solution)/shard_map/ppermute | solution.py:122
  87.7 12.5 %copy-start = (f32[128]{0:T(128)S(1)}, f32[128]{0:T(128)}, u32[]{:S(2)}) copy-start(f32[128]{0:T(128)} %param.9) | copy-start | bytes 1540
  87.7 12.4 %copy-start.1 = (f32[128]{0:T(128)S(1)}, f32[128]{0:T(128)}, u32[]{:S(2)}) copy-start(f32[128]{0:T(128)} %param.10) | copy-start | bytes 1540
  87.7 12.4 %collective-permute-start.7 = (f32[256,256]{1,0:T(8,128)S(1)}, f32[256,256]{1,0:T(8,128)S(1)}, u32[]{:S(2)}, u32[]{:S(2)}) collective-permute-start(f32[256,256]{1,0:T(8,128)S(1)} %shard_map.79.own), channel_id=1, source_target_pairs={{0,1},{1,0},{2,3},{3,2},{4,5},{5,4},{6,7},{7,6},{8,9},{9,8},{10,11... | collective-permute-start | bytes 786440 | tf_op jit(solution)/shard_map/ppermute | solution.py:169
